TPU v7x, 256 devices: a whole 4x4x8 slice. The times are simulated.
256 devices in a mesh: spec: 4 (over x), wave: 64 (over y, z, core).
Axes of the slice: x: 4, y: 4, z: 8, core: 2. Of those that a mesh axis runs over, the one named last changes fastest.
Arguments:
- pixels: float32 [8, 8, 3200, 500], P(None, 'spec', 'wave')
- ivar: float32 [8, 8, 3200, 500], P(None, 'spec', 'wave'), may hold values from 0.25 to 4
- mask: int32 [8, 8, 3200, 500], P(None, 'spec', 'wave'), may hold values 0 or 1
- psf_left: float32 [8, 8, 3200, 500], P(None, 'spec', 'wave'), may hold values from 0.1 to 0.45
- psf_right: float32 [8, 8, 3200, 500], P(None, 'spec', 'wave'), may hold values from 0.1 to 0.45
- sky_index: int32 [8, 40], P('spec'), may hold values from 0 to 499, as said below
Outputs:
- cleaned: float32 [8, 8, 3200, 500], P(None, 'spec', 'wave')
- sky_model: float32 [8, 3200], P(None, 'wave')
Inputs may be any that keep to these rules, and one draw needn't show every extreme that they name: `sky_index`: each row names 40 different fibres.
All inputs are finite; a program needn't handle non-finite values. No bound on the sum of `mask` on one device may be relied on, other than what follows from the above.
Results may differ from a plain program's by a relative error of at most 0.0002.
Values sent between devices are 32-bit elements; how exact they have to be, the bound alone decides.
A program may use at most 128 MiB of HBM per device.

v0:
```python
import jax
import jax.numpy as jnp
from jax import lax
from jax.sharding import PartitionSpec as P

F = 500


REG = 0.05
RIDGE = 1.0


def extended_2(cells, sides, width):
    for axis, dim in sides:
        count = lax.axis_size(axis)
        ends = count - 1
        head = lax.slice_in_dim(cells, 0, width, axis=dim)
        tail = lax.slice_in_dim(cells, cells.shape[dim] - width, cells.shape[dim], axis=dim)
        cells = jnp.concatenate(
            [
                lax.ppermute(tail, axis, [(i, (i + 1) % count) for i in range(ends)]),
                cells,
                lax.ppermute(head, axis, [((i + 1) % count, i) for i in range(ends)]),
            ],
            axis=dim,
        )
    return cells


def shift_up(values):
    return jnp.concatenate([values[1:], jnp.zeros_like(values[:1])], axis=0)


def shift_down(values):
    return jnp.concatenate([jnp.zeros_like(values[:1]), values[:-1]], axis=0)


def band_terms(pixel_rows, weight, left, right):
    diag_main = weight + shift_up(weight * left * left) + shift_down(weight * right * right) + REG
    first_off = weight * right + shift_up(weight * left)
    second_off = shift_up(weight * left * right)
    rhs_rows = (
        weight * pixel_rows
        + shift_up(weight * left * pixel_rows)
        + shift_down(weight * right * pixel_rows)
    )
    return (diag_main, first_off, second_off, rhs_rows)


def band_factor(diag_main, first_off, second_off):
    length = diag_main.shape[0]
    unit_fill = jnp.ones_like(diag_main[0])
    zero_fill = jnp.zeros_like(diag_main[0])
    pivots, lowers, farther = ([], [], [])
    pivot_last, pivot_before, lower_last = (unit_fill, unit_fill, zero_fill)
    for step_row in range(length):
        prev_one = first_off[step_row - 1] if step_row >= 1 else zero_fill
        prev_two = second_off[step_row - 2] if step_row >= 2 else zero_fill
        far_term = prev_two / pivot_before
        lower_term = (prev_one - far_term * lower_last) / pivot_last
        pivot_now = jnp.sqrt(diag_main[step_row] - lower_term * lower_term - far_term * far_term)
        pivots.append(pivot_now)
        lowers.append(lower_term)
        farther.append(far_term)
        pivot_before, pivot_last = (pivot_last, pivot_now)
        lower_last = lower_term
    return (pivots, lowers, farther)


def band_substitute(factors, rhs_rows):
    pivots, lowers, farther = factors
    length = len(pivots)
    zero_fill = jnp.zeros_like(rhs_rows[0])
    forward = []
    forward_last, forward_before = (zero_fill, zero_fill)
    for step_row in range(length):
        forward_now = (
            rhs_rows[step_row]
            - lowers[step_row] * forward_last
            - farther[step_row] * forward_before
        ) / pivots[step_row]
        forward.append(forward_now)
        forward_before, forward_last = (forward_last, forward_now)
    solved = [None] * length
    next_one, next_two = (zero_fill, zero_fill)
    for step_row in reversed(range(length)):
        result_now = forward[step_row]
        if step_row + 1 < length:
            result_now = result_now - lowers[step_row + 1] * next_one
        if step_row + 2 < length:
            result_now = result_now - farther[step_row + 2] * next_two
        result_now = result_now / pivots[step_row]
        solved[step_row] = result_now
        next_two, next_one = (next_one, result_now)
    return jnp.stack(solved)


def band_solve(pixel_rows, weight, left, right):
    diag_main, first_off, second_off, rhs_rows = band_terms(pixel_rows, weight, left, right)
    factors = band_factor(diag_main, first_off, second_off)
    return (band_substitute(factors, rhs_rows), diag_main)


def local(pixels, ivar, mask, psf_left, psf_right, sky_index):
    weight = ivar * (1.0 - mask.astype(jnp.float32))
    stacked = jnp.stack([pixels, weight, psf_left, psf_right])
    rows_here = pixels.shape[2]
    extended = extended_2(stacked, (("wave", 3),), 4)
    full_rows = jnp.moveaxis(extended, 3, 1)
    solved_all, diag_main = band_solve(full_rows[0], full_rows[1], full_rows[2], full_rows[3])
    solved = solved_all[4 : 4 + rows_here]
    diag_kept = diag_main[4 : 4 + rows_here]
    flux = jnp.moveaxis(solved, 0, 2)
    precision = jnp.moveaxis(diag_kept, 0, 2)
    is_sky = jnp.sum(
        (sky_index[:, :, None] == jnp.arange(F)[None, None, :]).astype(jnp.float32), axis=1
    )
    numer = jnp.einsum("eswf,sf->ew", precision * flux, is_sky, precision=lax.Precision.HIGHEST)
    denom = jnp.einsum("eswf,sf->ew", precision, is_sky, precision=lax.Precision.HIGHEST)
    numer, denom = lax.psum((numer, denom), "spec")
    sky_model = numer / denom
    total_rows = rows_here * lax.axis_size("wave")
    offsets = lax.axis_index("wave") * rows_here + jnp.arange(rows_here)
    position = 2.0 * offsets.astype(jnp.float32) / (total_rows - 1) - 1.0
    square = sky_model * sky_model
    moments = jnp.stack(
        [
            jnp.sum(square, axis=1),
            jnp.sum(square * position, axis=1),
            jnp.sum(square * position * position, axis=1),
        ],
        axis=1,
    )
    first_sum = jnp.einsum("eswf,ew->esf", flux, sky_model, precision=lax.Precision.HIGHEST)
    second_sum = jnp.einsum(
        "eswf,ew->esf", flux, sky_model * position, precision=lax.Precision.HIGHEST
    )
    fibre_sums = jnp.stack([first_sum, second_sum])
    moments, fibre_sums = lax.psum((moments, fibre_sums), "wave")
    upper_left = (moments[:, 0] + RIDGE)[:, None, None]
    lower_right = (moments[:, 2] + RIDGE)[:, None, None]
    cross = moments[:, 1][:, None, None]
    determinant = upper_left * lower_right - cross * cross
    slope_a = (lower_right * fibre_sums[0] - cross * fibre_sums[1]) / determinant
    slope_b = (upper_left * fibre_sums[1] - cross * fibre_sums[0]) / determinant
    fitted = (
        slope_a[:, :, None, :] + slope_b[:, :, None, :] * position[None, None, :, None]
    ) * sky_model[:, None, :, None]
    cleaned = flux - fitted
    return (cleaned, sky_model)


def solution(mesh):
    in_specs = (
        P(None, "spec", "wave", None),
        P(None, "spec", "wave", None),
        P(None, "spec", "wave", None),
        P(None, "spec", "wave", None),
        P(None, "spec", "wave", None),
        P("spec", None),
    )
    out_specs = (P(None, "spec", "wave", None), P(None, "wave"))
    return jax.shard_map(local, mesh=mesh, in_specs=in_specs, out_specs=out_specs, check_vma=False)
```

profile of v0, /device:TPU:1, one launch (start us, length us, event | category | flops | bytes accessed | tf_op | source)
XLA Modules:
  0.0 323.8 jit_solution(10945786833096671010)
XLA Ops:
  0.7 3.0 copy_bitcast_fusion.3
  3.7 0.3 copy-done.11
  4.0 1.6 fusion.9
  5.6 1.1 copy-done.8
  6.8 1.1 pad_maximum_fusion.3
  7.9 4.9 %collective-permute-start = (f32[4,8,2,4,500]{4,1,3,2,0:T(8,128)}, f32[4,8,2,4,500]{4,1,3,2,0:T(8,128)}, u32[]{:S(2)}, u32[]{:S(2)}) collective-permute-start(f32[4,8,2,4,500]{4,1,3,2,0:T(8,128)} %get-tuple-element.410), channel_id=1, source_target_pairs={{0,1},{1,2},{2,3},{3,4},{4,5},{5,6},{6,7},{7,8},{8,9},{9,10},{10,1... | collective-permute-start | bytes 1536008 | tf_op jit(solution)/shard_map/ppermute | solution.py:21
  12.8 2.3 collective-permute-start.1
  15.1 0.1 convert_reduce_fusion
  15.3 4.0 %collective-permute-done = f32[4,8,2,4,500]{4,1,3,2,0:T(8,128)} collective-permute-done((f32[4,8,2,4,500]{4,1,3,2,0:T(8,128)}, f32[4,8,2,4,500]{4,1,3,2,0:T(8,128)}, u32[]{:S(2)}, u32[]{:S(2)}) %collective-permute-start) | collective-permute-done | bytes 512032 | tf_op jit(solution)/shard_map/ppermute | solution.py:21
  19.2 4.4 %collective-permute-done.1 = f32[4,8,2,4,500]{4,1,3,2,0:T(8,128)} collective-permute-done((f32[4,8,2,4,500]{4,1,3,2,0:T(8,128)}, f32[4,8,2,4,500]{4,1,3,2,0:T(8,128)}, u32[]{:S(2)}, u32[]{:S(2)}) %collective-permute-start.1) | collective-permute-done | bytes 512032 | tf_op jit(solution)/shard_map/ppermute | solution.py:23
  23.6 2.9 maximum_bitcast_fusion
  26.6 0.9 fusion.592
  27.5 0.2 copy.590
  27.7 0.2 copy.589
  27.9 0.7 copy_multiply_fusion.1
  28.6 0.9 slice_multiply_fusion.2
  29.5 0.9 pad_add_fusion.1
  30.4 0.5 slice_multiply_fusion.1
  30.9 0.4 copy_multiply_fusion
  31.3 1.2 pad_add_fusion.2
  32.5 0.5 fusion
  32.9 0.1 slice_bitcast_fusion.1
  33.1 0.1 fusion.24
  33.1 0.1 subtract_divide_fusion.113
  33.3 0.1 subtract_divide_fusion.111
  33.4 0.1 fusion.394
  33.5 1.0 fusion.277
  34.6 1.0 subtract_divide_fusion.186
  35.6 0.4 subtract_divide_fusion.163
  36.1 0.4 constant_dynamic-update-slice_fusion.49
  36.7 1.0 subtract_divide_fusion.109
  37.7 1.1 subtract_divide_fusion.107
  38.9 1.0 subtract_divide_fusion.105
  39.9 1.0 subtract_divide_fusion.103
  40.9 1.1 subtract_divide_fusion.101
  42.1 1.0 subtract_divide_fusion.99
  43.1 1.1 subtract_divide_fusion.97
  44.3 1.0 subtract_divide_fusion.95
  45.3 1.1 subtract_divide_fusion.93
  46.5 1.0 subtract_divide_fusion.91
  47.5 0.2 subtract_divide_fusion.75
  47.8 1.0 subtract_divide_fusion.28
  48.7 0.8 subtract_divide_fusion.26
  49.6 1.0 subtract_divide_fusion.24
  50.6 0.8 subtract_divide_fusion.22
  51.4 0.8 subtract_divide_fusion.20
  52.2 0.8 subtract_divide_fusion.18
  53.0 0.8 subtract_divide_fusion.16
  53.8 0.8 subtract_divide_fusion.14
  54.6 0.8 subtract_divide_fusion.12
  55.4 0.8 subtract_divide_fusion.10
  56.3 0.1 constant_dynamic-update-slice_fusion.26
  56.8 0.4 bitcast_multiply_fusion.5
  57.1 3.3 %fusion.3 = f32[1,8,50,1]{2,0,3,1:T(1,128)S(1)} fusion(f32[8,2,50,500]{3,0,2,1:T(8,128)S(1)} %bitcast_multiply_fusion.5, f32[2,500,1,1]{1,0,2,3:T(2,128)S(1)} %bitcast.2827), kind=kOutput, calls=%fused_computation.16 | convolution fusion | flops 4800000 | bytes 1605600 | tf_op jit(solution)/shard_map/eswf,sf->ew/dot_general | solution.py:118
  60.4 3.3 %fusion.1 = f32[1,8,50,1]{2,0,3,1:T(1,128)S(1)} fusion(f32[8,2,50,500]{3,0,2,1:T(8,128)S(1)} %slice_bitcast_fusion.1, f32[2,500,1,1]{1,0,2,3:T(2,128)S(1)} %bitcast.2828), kind=kOutput, calls=%fused_computation.14 | convolution fusion | flops 4800000 | bytes 1605600 | tf_op jit(solution)/shard_map/eswf,sf->ew/dot_general | solution.py:119
  63.7 8.6 %all-reduce.6 = (f32[8,50]{1,0:T(8,128)S(1)}, f32[8,50]{1,0:T(8,128)S(1)}) all-reduce(f32[8,50]{1,0:T(8,128)S(1)} %bitcast.2829, f32[8,50]{1,0:T(8,128)S(1)} %bitcast.2830), channel_id=1, replica_groups=mesh['spec'=4,'wave'=64] {'spec'}, use_global_device_ids=true, to_apply=%region_1.0 | all-reduce | flops 800 | bytes 6400 | tf_op jit(solution)/shard_map/psum | solution.py:120
  72.3 0.2 multiply_reduce_fusion.1
  72.5 2.0 fusion.7
  74.5 2.0 fusion.5
  76.6 244.2 %all-reduce.5 = (f32[2,8,2,500]{3,1,2,0:T(8,128)S(1)}, f32[8,3]{0,1:T(4,128)S(1)}) all-reduce(f32[2,8,2,500]{3,1,2,0:T(8,128)S(1)} %pad_maximum_fusion.4, f32[8,3]{0,1:T(4,128)S(1)} %pad_maximum_fusion.5), channel_id=1, replica_groups=mesh['spec'=4,'wave'=64] {'wave'}, use_global_device_ids=true, to_apply=%region_7.0 | all-reduce | flops 16024 | bytes 128192 | tf_op jit(solution)/shard_map/psum | solution.py:139
  320.9 0.1 copy.466
  320.9 0.1 subtract_divide_fusion.1
  321.0 0.3 multiply_subtract_fusion
  321.4 2.4 copy.467
  (88 shorter events, 0.5 us)
Async XLA Ops:
  0.6 3.1 copy-start.12
  0.6 3.1 copy-start.10
  0.7 3.4 %copy-start.11 = (s32[8,2,50,500]{3,1,2,0:T(2,128)S(1)}, s32[8,2,50,500]{3,1,2,0:T(2,128)}, u32[]{:S(2)}) copy-start(s32[8,2,50,500]{3,1,2,0:T(2,128)} %param.8) | copy-start | bytes 4800004
  5.6 1.2 copy-start.8
  5.6 2.3 copy-start.9
  6.8 8.4 %copy-start.14 = (s32[2,40]{1,0:T(2,128)S(1)}, s32[2,40]{1,0:T(2,128)}, u32[]{:S(2)}) copy-start(s32[2,40]{1,0:T(2,128)} %param.11) | copy-start | bytes 964
  7.9 11.4 %collective-permute-start = (f32[4,8,2,4,500]{4,1,3,2,0:T(8,128)}, f32[4,8,2,4,500]{4,1,3,2,0:T(8,128)}, u32[]{:S(2)}, u32[]{:S(2)}) collective-permute-start(f32[4,8,2,4,500]{4,1,3,2,0:T(8,128)} %get-tuple-element.410), channel_id=1, source_target_pairs={{0,1},{1,2},{2,3},{3,4},{4,5},{5,6},{6,7},{7,8},{8,9},{9,10},{10,1... | collective-permute-start | bytes 1536008 | tf_op jit(solution)/shard_map/ppermute | solution.py:21
  12.8 10.8 %collective-permute-start.1 = (f32[4,8,2,4,500]{4,1,3,2,0:T(8,128)}, f32[4,8,2,4,500]{4,1,3,2,0:T(8,128)}, u32[]{:S(2)}, u32[]{:S(2)}) collective-permute-start(f32[4,8,2,4,500]{4,1,3,2,0:T(8,128)} %get-tuple-element.411), channel_id=1, source_target_pairs={{1,0},{2,1},{3,2},{4,3},{5,4},{6,5},{7,6},{8,7},{9,8},{10,9},{11,1... | collective-permute-start | bytes 1536008 | tf_op jit(solution)/shard_map/ppermute | solution.py:23
  28.6 7.5 %copy-start.2 = (f32[58,8,2,500]{3,1,2,0:T(8,128)}, f32[58,8,2,500]{3,1,2,0:T(8,128)S(1)}, u32[]{:S(2)}) copy-start(f32[58,8,2,500]{3,1,2,0:T(8,128)S(1)} %get-tuple-element.402) | copy-start | bytes 5568004
  30.4 4.2 %copy-start.6 = (f32[58,8,2,500]{3,1,2,0:T(8,128)}, f32[58,8,2,500]{3,1,2,0:T(8,128)S(1)}, u32[]{:S(2)}) copy-start(f32[58,8,2,500]{3,1,2,0:T(8,128)S(1)} %get-tuple-element.404) | copy-start | bytes 5568004
  32.5 2.1 copy-start.4
  32.9 1.6 copy-start
  37.7 9.8 %copy-start.7 = (f32[58,8,2,500]{3,1,2,0:T(8,128)S(1)}, f32[58,8,2,500]{3,1,2,0:T(8,128)}, u32[]{:S(2)}) copy-start(f32[58,8,2,500]{3,1,2,0:T(8,128)} %copy-done.6) | copy-start | bytes 5568004
  40.9 6.6 %copy-start.3 = (f32[58,8,2,500]{3,1,2,0:T(8,128)S(1)}, f32[58,8,2,500]{3,1,2,0:T(8,128)}, u32[]{:S(2)}) copy-start(f32[58,8,2,500]{3,1,2,0:T(8,128)} %copy-done.2) | copy-start | bytes 5568004
  43.1 4.4 %copy-start.1 = (f32[58,8,2,500]{3,1,0,2:T(8,128)S(1)}, f32[58,8,2,500]{3,1,0,2:T(8,128)}, u32[]{:S(2)}) copy-start(f32[58,8,2,500]{3,1,0,2:T(8,128)} %copy-done) | copy-start | bytes 5568004
  45.3 2.4 copy-start.5
  72.5 248.4 %copy-start.13 = (f32[8,50]{1,0:T(8,128)}, f32[8,50]{1,0:T(8,128)S(1)}, u32[]{:S(2)}) copy-start(f32[8,50]{1,0:T(8,128)S(1)} %get-tuple-element.11) | copy-start | bytes 4804
where the time goes:
time: 327 us; the launch traced here: 324 us
  blocking collectives  253 us (77%)
  other arithmetic  34.4 us (11%)
  matrix products  10.7 us (3%)
  local copies, waits for them, and re-layouts  8.75 us (3%)
  waiting for transfers between devices  8.39 us (3%)
  starting transfers between devices  7.21 us (2%)
    psum x1, blocking collectives, local(): moments, fibre_sums = lax.psum((moments, fibre_sums), 'wave')  244 us
    div x12, other arithmetic, band_substitute(): (rhs_rows[step_row] - lowers[step_row] * forward_last - farther[step_row]...  10.9 us
    div x16, other arithmetic, band_substitute(): result_now = result_now / pivots[step_row]  10 us
    psum x1, blocking collectives, local(): numer, denom = lax.psum((numer, denom), 'spec')  8.58 us
  transfers between devices with their start and end apart: 2, of which 2 were waited for; matrix products, arithmetic and copies ran while one was open for 0% of the time, Pallas kernels for 0%

commit v1 on v0

--- a/solution.py
+++ b/solution.py
@@ -1,9 +1,13 @@
 import jax
 import jax.numpy as jnp
 from jax import lax
+from jax.experimental import pallas as pl
+from jax.experimental.pallas import tpu as pltpu
 from jax.sharding import PartitionSpec as P
 
 F = 500
+PADDED = 512
+EXPO = 8
 
 
 REG = 0.05
@@ -25,6 +29,157 @@
             axis=dim,
         )
     return cells
+
+
+MESH = pl.DeviceIdType.MESH
+ROWS = 4
+COLS = 8
+CORES = 2
+PLANE = ROWS * CORES
+
+
+def spec_kernel(mine, total, inbox, send_sem, recv_sem):
+    me = lax.axis_index("spec")
+    count = lax.axis_size("spec")
+    barrier = pltpu.get_barrier_semaphore()
+    peers = [lax.rem(me + d, count) for d in range(1, count)]
+    for peer in peers:
+        pl.semaphore_signal(barrier, inc=1, device_id={"spec": peer}, device_id_type=MESH)
+    pl.semaphore_wait(barrier, count - 1)
+    copies = []
+    for d, peer in enumerate(peers, 1):
+        copies.append(
+            pltpu.make_async_remote_copy(
+                src_ref=mine,
+                dst_ref=inbox.at[count - 1 - d],
+                send_sem=send_sem.at[d - 1],
+                recv_sem=recv_sem.at[count - 1 - d],
+                device_id={"spec": peer},
+                device_id_type=MESH,
+            )
+        )
+        copies[-1].start()
+    for copy in copies:
+        copy.wait()
+    total[...] = mine[...] + inbox[0] + inbox[1] + inbox[2]
+
+
+def spec_sum(mine):
+    count = lax.axis_size("spec")
+    return pl.pallas_call(
+        spec_kernel,
+        out_shape=jax.ShapeDtypeStruct(mine.shape, mine.dtype),
+        in_specs=[pl.BlockSpec(memory_space=pltpu.VMEM)],
+        out_specs=pl.BlockSpec(memory_space=pltpu.VMEM),
+        scratch_shapes=[
+            pltpu.VMEM((count - 1,) + mine.shape, mine.dtype),
+            pltpu.SemaphoreType.DMA((count - 1,)),
+            pltpu.SemaphoreType.DMA((count - 1,)),
+        ],
+        compiler_params=pltpu.CompilerParams(collective_id=1, has_side_effects=True),
+        name="spec_sum",
+    )(mine)
+
+
+def wave_kernel(mine, total, box_a, box_b, part, whole, send_a, send_b, send_c, recv_a, recv_b, recv_c):
+    me = lax.axis_index("wave")
+    core = lax.rem(me, CORES)
+    col = lax.rem(lax.div(me, CORES), COLS)
+    row = lax.div(me, CORES * COLS)
+    mem = row * CORES + core
+    wide = mine.shape[0] // PLANE
+
+    def plane_peer(d):
+        other = lax.rem(mem + d, PLANE)
+        return other, (lax.div(other, CORES) * COLS + col) * CORES + lax.rem(other, CORES)
+
+    def line_peer(d):
+        return (row * COLS + lax.rem(col + d, COLS)) * CORES + core
+
+    barrier = pltpu.get_barrier_semaphore()
+    for d in range(1, PLANE):
+        pl.semaphore_signal(barrier, inc=1, device_id={"wave": plane_peer(d)[1]}, device_id_type=MESH)
+    for d in range(1, COLS):
+        pl.semaphore_signal(barrier, inc=1, device_id={"wave": line_peer(d)}, device_id_type=MESH)
+    pl.semaphore_wait(barrier, PLANE - 1 + COLS - 1)
+
+    first, second, third = [], [], []
+    for d in range(1, PLANE):
+        other, where = plane_peer(d)
+        first.append(
+            pltpu.make_async_remote_copy(
+                src_ref=mine.at[pl.ds(other * wide, wide)],
+                dst_ref=box_a.at[PLANE - 1 - d],
+                send_sem=send_a.at[d - 1],
+                recv_sem=recv_a.at[PLANE - 1 - d],
+                device_id={"wave": where},
+                device_id_type=MESH,
+            )
+        )
+        first[-1].start()
+    for copy in first:
+        copy.wait_recv()
+    acc = mine[pl.ds(mem * wide, wide)]
+    for d in range(PLANE - 1):
+        acc = acc + box_a[d]
+    part[...] = acc
+    for d in range(1, COLS):
+        second.append(
+            pltpu.make_async_remote_copy(
+                src_ref=part,
+                dst_ref=box_b.at[COLS - 1 - d],
+                send_sem=send_b.at[d - 1],
+                recv_sem=recv_b.at[COLS - 1 - d],
+                device_id={"wave": line_peer(d)},
+                device_id_type=MESH,
+            )
+        )
+        second[-1].start()
+    for copy in second:
+        copy.wait_recv()
+    acc = part[...]
+    for d in range(COLS - 1):
+        acc = acc + box_b[d]
+    whole[...] = acc
+    total[pl.ds(mem * wide, wide)] = acc
+    for d in range(1, PLANE):
+        third.append(
+            pltpu.make_async_remote_copy(
+                src_ref=whole,
+                dst_ref=total.at[pl.ds(mem * wide, wide)],
+                send_sem=send_c.at[d - 1],
+                recv_sem=recv_c.at[PLANE - 1 - d],
+                device_id={"wave": plane_peer(d)[1]},
+                device_id_type=MESH,
+            )
+        )
+        third[-1].start()
+    for copy in third:
+        copy.wait_recv()
+    for copy in first + second + third:
+        copy.wait_send()
+
+
+def wave_sum(mine):
+    wide = mine.shape[0] // PLANE
+    piece = (wide,) + mine.shape[1:]
+    sems = [pltpu.SemaphoreType.DMA((PLANE - 1,)), pltpu.SemaphoreType.DMA((COLS - 1,)), pltpu.SemaphoreType.DMA((PLANE - 1,))]
+    return pl.pallas_call(
+        wave_kernel,
+        out_shape=jax.ShapeDtypeStruct(mine.shape, mine.dtype),
+        in_specs=[pl.BlockSpec(memory_space=pltpu.VMEM)],
+        out_specs=pl.BlockSpec(memory_space=pltpu.VMEM),
+        scratch_shapes=[
+            pltpu.VMEM((PLANE - 1,) + piece, mine.dtype),
+            pltpu.VMEM((COLS - 1,) + piece, mine.dtype),
+            pltpu.VMEM(piece, mine.dtype),
+            pltpu.VMEM(piece, mine.dtype),
+        ]
+        + sems
+        + sems,
+        compiler_params=pltpu.CompilerParams(collective_id=2, has_side_effects=True),
+        name="wave_sum",
+    )(mine)
 
 
 def shift_up(values):
@@ -117,7 +272,8 @@
     )
     numer = jnp.einsum("eswf,sf->ew", precision * flux, is_sky, precision=lax.Precision.HIGHEST)
     denom = jnp.einsum("eswf,sf->ew", precision, is_sky, precision=lax.Precision.HIGHEST)
-    numer, denom = lax.psum((numer, denom), "spec")
+    both = spec_sum(jnp.stack([numer, denom]))
+    numer, denom = both[0], both[1]
     sky_model = numer / denom
     total_rows = rows_here * lax.axis_size("wave")
     offsets = lax.axis_index("wave") * rows_here + jnp.arange(rows_here)
@@ -136,7 +292,10 @@
         "eswf,ew->esf", flux, sky_model * position, precision=lax.Precision.HIGHEST
     )
     fibre_sums = jnp.stack([first_sum, second_sum])
-    moments, fibre_sums = lax.psum((moments, fibre_sums), "wave")
+    tail = jnp.zeros((2, EXPO, 2, PADDED - F), jnp.float32).at[0, :, 0, :3].set(moments)
+    packed = jnp.concatenate([fibre_sums, tail], axis=3)
+    packed = wave_sum(packed.reshape(2 * EXPO, 2, PADDED)).reshape(2, EXPO, 2, PADDED)
+    moments, fibre_sums = packed[0, :, 0, F : F + 3], packed[..., :F]
     upper_left = (moments[:, 0] + RIDGE)[:, None, None]
     lower_right = (moments[:, 2] + RIDGE)[:, None, None]
     cross = moments[:, 1][:, None, None]

time: 327 us -> 104 us (0.32)
  blocking collectives: 253 us -> 0 us
  Pallas kernels: 0 us -> 27.7 us
    psum x2 -> x0, blocking collectives: 253 us -> none  [the longest x1 244 us: local(): moments, fibre_sums = lax.psum((moments, fibre_sums), 'wave')]
    pallas_call x0 -> x2, Pallas kernels: none -> 27.7 us  [the longest x1 21.6 us: wave_sum(): pl.pallas_call(wave_kernel, out_shape=jax.ShapeDtypeStruct(mine.shape, mi...]
where the time goes in v1:
time: 104 us; the launch traced here: 103 us
  other arithmetic  37.5 us (36%)
  Pallas kernels  27.7 us (27%)
  matrix products  10.7 us (10%)
  local copies, waits for them, and re-layouts  9.45 us (9%)
  waiting for transfers between devices  8.39 us (8%)
  starting transfers between devices  7.22 us (7%)
  between operations  1.62 us (2%)
    pallas_call x1, Pallas kernels, wave_sum(): pl.pallas_call(wave_kernel, out_shape=jax.ShapeDtypeStruct(mine.shape, mi...  21.6 us
    div x12, other arithmetic, band_substitute(): (rhs_rows[step_row] - lowers[step_row] * forward_last - farther[step_row]...  10.9 us
    div x16, other arithmetic, band_substitute(): result_now = result_now / pivots[step_row]  10 us
    pallas_call x1, Pallas kernels, spec_sum(): pl.pallas_call(spec_kernel, out_shape=jax.ShapeDtypeStruct(mine.shape, mi...  6.13 us
    ppermute x1, starting transfers between devices, extended_2(): lax.ppermute(tail, axis, [(i, (i + 1) % count) for i in range(ends)])  4.92 us
    unnamed x84, local copies, waits for them, and re-layouts  4.46 us
    ppermute x1, waiting for transfers between devices, extended_2(): lax.ppermute(head, axis, [((i + 1) % count, i) for i in range(ends)])  4.4 us
    ppermute x1, waiting for transfers between devices, extended_2(): lax.ppermute(tail, axis, [(i, (i + 1) % count) for i in range(ends)])  3.99 us
  transfers between devices with their start and end apart: 2, of which 2 were waited for; matrix products, arithmetic and copies ran while one was open for 0% of the time, Pallas kernels for 0%

profile of v1, /device:TPU:1, one launch (start us, length us, event | category | flops | bytes accessed | tf_op | source)
XLA Modules:
  0.0 102.6 jit_solution(10178688409180587313)
XLA Ops:
  0.7 3.0 %copy_bitcast_fusion.3 = (f32[1,8,2,50,500]{4,1,3,2,0:T(8,128)S(1)}, f32[1,8,2,50,500]{4,1,3,2,0:T(8,128)S(1)}) fusion(f32[8,2,50,500]{3,1,2,0:T(2,128)} %param.12, f32[8,2,50,500]{3,1,2,0:T(2,128)} %param.11), kind=kLoop, calls=%fused_computation.25 | loop fusion | bytes 6400000 | tf_op jit(solution)/shard_map/stack | solution.py:261
  3.7 0.3 copy-done.10
  4.0 1.6 %fusion.9 = (f32[1,8,2,50,500]{4,1,3,2,0:T(8,128)S(1)}, f32[1,8,2,50,500]{4,1,3,2,0:T(8,128)S(1)}) fusion(f32[8,2,50,500]{3,1,2,0:T(2,128)S(1)} %copy-done.10, s32[8,2,50,500]{3,1,2,0:T(2,128)S(1)} %copy-done.11, f32[8,2,50,500]{3,1,2,0:T(2,128)S(1)} %copy-done.12), kind=kLoop, calls=%fused_computation.28 | loop fusion | flops 1200000 | bytes 8000000 | tf_op jit(solution)/shard_map/stack | solution.py:261
  5.7 1.2 %pad_maximum_fusion.3 = (f32[4,8,2,4,500]{4,1,3,2,0:T(8,128)}, f32[4,8,2,4,500]{4,1,3,2,0:T(8,128)}) fusion(f32[1,8,2,50,500]{4,1,3,2,0:T(8,128)S(1)} %get-tuple-element.433, f32[1,8,2,50,500]{4,1,3,2,0:T(8,128)S(1)} %get-tuple-element.434, f32[1,8,2,50,500]{4,1,3,2,0:T(8,128)S(1)} %get-tuple-element.435, f32[1,8,2,50,500]{4,1,3,2,0:T(8,128)S(1)} %get-tuple-element.436), kind=kLoop, calls=%fused_computation.37 | loop fusion | flops 768000 | bytes 7424000 | tf_op jit(solution)/shard_map/slice | solution.py:22
  6.9 0.3 copy-done.8
  7.1 0.6 copy-done.9
  7.7 4.9 %collective-permute-start = (f32[4,8,2,4,500]{4,1,3,2,0:T(8,128)}, f32[4,8,2,4,500]{4,1,3,2,0:T(8,128)}, u32[]{:S(2)}, u32[]{:S(2)}) collective-permute-start(f32[4,8,2,4,500]{4,1,3,2,0:T(8,128)} %get-tuple-element.417), channel_id=1, source_target_pairs={{0,1},{1,2},{2,3},{3,4},{4,5},{5,6},{6,7},{7,8},{8,9},{9,10},{10,1... | collective-permute-start | bytes 1536008 | tf_op jit(solution)/shard_map/ppermute | solution.py:25
  12.6 2.3 %collective-permute-start.1 = (f32[4,8,2,4,500]{4,1,3,2,0:T(8,128)}, f32[4,8,2,4,500]{4,1,3,2,0:T(8,128)}, u32[]{:S(2)}, u32[]{:S(2)}) collective-permute-start(f32[4,8,2,4,500]{4,1,3,2,0:T(8,128)} %get-tuple-element.418), channel_id=1, source_target_pairs={{1,0},{2,1},{3,2},{4,3},{5,4},{6,5},{7,6},{8,7},{9,8},{10,9},{11,1... | collective-permute-start | bytes 1536008 | tf_op jit(solution)/shard_map/ppermute | solution.py:27
  15.1 4.0 %collective-permute-done = f32[4,8,2,4,500]{4,1,3,2,0:T(8,128)} collective-permute-done((f32[4,8,2,4,500]{4,1,3,2,0:T(8,128)}, f32[4,8,2,4,500]{4,1,3,2,0:T(8,128)}, u32[]{:S(2)}, u32[]{:S(2)}) %collective-permute-start) | collective-permute-done | bytes 512032 | tf_op jit(solution)/shard_map/ppermute | solution.py:25
  19.1 4.4 %collective-permute-done.1 = f32[4,8,2,4,500]{4,1,3,2,0:T(8,128)} collective-permute-done((f32[4,8,2,4,500]{4,1,3,2,0:T(8,128)}, f32[4,8,2,4,500]{4,1,3,2,0:T(8,128)}, u32[]{:S(2)}, u32[]{:S(2)}) %collective-permute-start.1) | collective-permute-done | bytes 512032 | tf_op jit(solution)/shard_map/ppermute | solution.py:27
  23.5 2.8 %maximum_bitcast_fusion = f32[4,58,8,2,500]{4,2,1,3,0:T(8,128)S(1)} fusion(f32[4,8,2,4,500]{4,1,3,2,0:T(8,128)} %collective-permute-done.1, f32[1,8,2,50,500]{4,1,3,2,0:T(8,128)S(1)} %get-tuple-element.433, f32[1,8,2,50,500]{4,1,3,2,0:T(8,128)S(1)} %get-tuple-element.434, f32[1,8,2,50,500]{4,1,3,2,0:T(8,128)} %copy-done.8, f32[1,8,2,50,500]{4,1,3,2,0:T(8,128)} %copy-done.9, ...), kind=kLoop, calls=%fused_computation | loop fusion | flops 9280000 | bytes 14848000 | tf_op jit(solution)/shard_map/transpose | solution.py:264
  26.3 0.9 fusion.593
  27.2 0.2 copy.600
  27.4 0.2 copy.599
  27.6 0.7 copy_multiply_fusion.1
  28.3 1.1 %slice_multiply_fusion.2 = (f32[57,8,2,500]{3,1,2,0:T(8,128)S(1)}, f32[57,8,2,500]{3,1,2,0:T(8,128)S(1)}, f32[57,8,2,500]{3,1,2,0:T(8,128)S(1)}) fusion(f32[58,8,2,500]{3,1,2,0:T(8,128)S(1)} %bitcast.2834, f32[58,8,2,500]{3,1,2,0:T(8,128)S(1)} %get-tuple-element.410, f32[58,8,2,500]{3,1,2,0:T(8,128)S(1)} %bitcast.2836), kind=kLoop, calls=%fused_computation.13 | loop fusion | flops 912000 | bytes 10944000 | tf_op jit(solution)/shard_map/mul | solution.py:199
  29.4 0.7 pad_add_fusion.1
  30.1 0.6 slice_multiply_fusion.1
  30.7 0.4 copy_multiply_fusion
  31.1 1.3 %pad_add_fusion.2 = (f32[58,8,2,500]{3,1,2,0:T(8,128)S(1)}, f32[58,8,2,500]{3,1,2,0:T(8,128)S(1)}) fusion(f32[57,8,2,500]{3,1,2,0:T(8,128)S(1)} %get-tuple-element.425, f32[57,8,2,500]{3,1,2,0:T(8,128)S(1)} %get-tuple-element.422, f32[1,58,8,2,500]{4,2,1,3,0:T(8,128)S(1)} %get-tuple-element.414, f32[1,58,8,2,500]{4,2,1,3,0:T(8,128)S(1)} %get-tuple-element.413, ...), kind=kLoop, calls=%fused_computation.9 | loop fusion | flops 1856000 | bytes 12896000 | tf_op jit(solution)/shard_map/add | solution.py:198
  32.4 0.5 fusion
  32.9 0.1 slice_bitcast_fusion.1
  33.1 0.1 subtract_divide_fusion.113
  33.3 0.1 fusion.395
  33.4 1.0 %fusion.278 = (f32[8,2,500]{2,0,1:T(8,128)S(1)}, f32[8,2,500]{2,0,1:T(8,128)S(1)}, f32[8,2,500]{2,0,1:T(8,128)S(1)}, f32[8,2,500]{2,0,1:T(8,128)S(1)}, f32[8,2,5...) fusion(f32[58,8,2,500]{3,1,2,0:T(8,128)S(1)} %get-tuple-element, ...), kind=kLoop, calls=%fused_computation.513 | loop fusion | flops 2504000 | bytes 6368000 | tf_op jit(solution)/shard_map/div | solution.py:215
  34.5 1.1 %subtract_divide_fusion.186 = (f32[8,2,500]{2,0,1:T(8,128)S(1)}, f32[8,2,500]{2,0,1:T(8,128)S(1)}, f32[8,2,500]{2,0,1:T(8,128)S(1)}, f32[8,2,500]{2,0,1:T(8,128)...) fusion(f32[58,8,2,500]{3,1,0,2:T(8,128)S(1)} %fusion, ...), kind=kLoop, calls=%fused_computation.967 | loop fusion | flops 3224000 | bytes 9024000 | tf_op jit(solution)/shard_map/div | solution.py:247
  35.6 0.4 subtract_divide_fusion.163
  36.0 0.4 constant_dynamic-update-slice_fusion.49
  36.7 1.0 subtract_divide_fusion.109
  37.7 1.1 %subtract_divide_fusion.107 = (f32[1,8,2,500]{3,1,2,0:T(8,128)S(1)}, f32[1,8,2,500]{3,1,2,0:T(8,128)S(1)}, f32[1,8,2,500]{3,1,2,0:T(8,128)S(1)}, f32[1,8,2,500]{...) fusion(f32[1,8,2,500]{3,1,2,0:T(8,128)S(1)} %get-tuple-element.167, ...), kind=kLoop, calls=%fused_computation.888 | loop fusion | flops 272000 | bytes 704000 | tf_op jit(solution)/shard_map/div | solution.py:232
  38.8 1.0 subtract_divide_fusion.105
  39.9 1.0 subtract_divide_fusion.103
  40.9 1.1 %subtract_divide_fusion.101 = (f32[1,8,2,500]{3,1,2,0:T(8,128)S(1)}, f32[1,8,2,500]{3,1,2,0:T(8,128)S(1)}, f32[1,8,2,500]{3,1,2,0:T(8,128)S(1)}, f32[1,8,2,500]{...) fusion(f32[1,8,2,500]{3,1,2,0:T(8,128)S(1)} %get-tuple-element.149, ...), kind=kLoop, calls=%fused_computation.882 | loop fusion | flops 272000 | bytes 704000 | tf_op jit(solution)/shard_map/div | solution.py:232
  42.0 1.0 subtract_divide_fusion.99
  43.1 1.1 %subtract_divide_fusion.97 = (f32[1,8,2,500]{3,1,2,0:T(8,128)S(1)}, f32[1,8,2,500]{3,1,2,0:T(8,128)S(1)}, f32[1,8,2,500]{3,1,2,0:T(8,128)S(1)}, f32[1,8,2,500]{3...) fusion(f32[1,8,2,500]{3,1,2,0:T(8,128)S(1)} %get-tuple-element.137, ...), kind=kLoop, calls=%fused_computation.878 | loop fusion | flops 272000 | bytes 704000 | tf_op jit(solution)/shard_map/div | solution.py:232
  44.2 1.0 subtract_divide_fusion.95
  45.3 1.1 %subtract_divide_fusion.93 = (f32[1,8,2,500]{3,1,2,0:T(8,128)S(1)}, f32[1,8,2,500]{3,1,2,0:T(8,128)S(1)}, f32[1,8,2,500]{3,1,2,0:T(8,128)S(1)}, f32[1,8,2,500]{3...) fusion(f32[1,8,2,500]{3,1,2,0:T(8,128)S(1)} %get-tuple-element.125, ...), kind=kLoop, calls=%fused_computation.874 | loop fusion | flops 272000 | bytes 704000 | tf_op jit(solution)/shard_map/div | solution.py:232
  46.4 1.0 subtract_divide_fusion.91
  47.5 0.2 subtract_divide_fusion.75
  47.7 1.0 subtract_divide_fusion.28
  48.7 0.8 subtract_divide_fusion.26
  49.5 1.0 subtract_divide_fusion.24
  50.5 0.8 subtract_divide_fusion.22
  51.3 0.8 subtract_divide_fusion.20
  52.1 0.8 subtract_divide_fusion.18
  53.0 0.8 subtract_divide_fusion.16
  53.8 0.8 subtract_divide_fusion.14
  54.6 0.8 subtract_divide_fusion.12
  55.4 0.8 subtract_divide_fusion.10
  56.7 0.4 bitcast_multiply_fusion.5
  57.1 3.3 %fusion.3 = f32[1,8,50,1]{2,0,3,1:T(1,128)S(1)} fusion(f32[8,2,50,500]{3,0,2,1:T(8,128)S(1)} %bitcast_multiply_fusion.5, f32[2,500,1,1]{1,0,2,3:T(2,128)S(1)} %bitcast.2842), kind=kOutput, calls=%fused_computation.16 | convolution fusion | flops 4800000 | bytes 1605600 | tf_op jit(solution)/shard_map/eswf,sf->ew/dot_general | solution.py:273
  60.3 3.3 %fusion.1 = f32[1,8,50,1]{2,0,3,1:T(1,128)S(1)} fusion(f32[8,2,50,500]{3,0,2,1:T(8,128)S(1)} %slice_bitcast_fusion.1, f32[2,500,1,1]{1,0,2,3:T(2,128)S(1)} %bitcast.2843), kind=kOutput, calls=%fused_computation.14 | convolution fusion | flops 4800000 | bytes 1605600 | tf_op jit(solution)/shard_map/eswf,sf->ew/dot_general | solution.py:274
  63.6 0.6 pad_maximum_fusion.4.mine
  64.3 6.1 %spec_sum.1 = f32[2,8,50]{2,1,0:T(8,128)} custom-call(f32[2,8,50]{2,1,0:T(8,128)} %pad_maximum_fusion.4.mine), custom_call_target="tpu_custom_call" | custom-call | tf_op jit(solution)/shard_map/spec_sum/pallas_call | solution.py:69
  70.4 0.8 slice_divide_fusion.58
  71.2 2.1 %fusion.7 = f32[8,1,2,500]{3,1,2,0:T(1,128)S(1)} fusion(f32[8,50,1,1]{1,2,3,0:T(1,128)S(1)} %bitcast.2845, f32[8,2,50,500]{3,0,2,1:T(8,128)S(1)} %bitcast.2832), kind=kOutput, calls=%fused_computation.20 | convolution fusion | flops 4800000 | bytes 1633600 | tf_op jit(solution)/shard_map/eswf,ew->esf/dot_general | solution.py:290
  73.3 0.2 multiply_reduce_fusion.1
  73.4 2.1 %fusion.5 = f32[8,1,2,500]{3,1,2,0:T(1,128)S(1)} fusion(f32[8,50,1,1]{1,2,3,0:T(1,128)S(1)} %bitcast.2844, f32[8,2,50,500]{3,0,2,1:T(8,128)S(1)} %bitcast.2833), kind=kOutput, calls=%fused_computation.18 | convolution fusion | flops 4800000 | bytes 1633600 | tf_op jit(solution)/shard_map/eswf,ew->esf/dot_general | solution.py:291
  75.6 0.7 fusion.12
  76.3 21.6 %wave_sum.1 = f32[16,2,512]{2,1,0:T(2,128)} custom-call(f32[16,2,512]{2,1,0:T(2,128)} %bitcast.2839), custom_call_target="tpu_custom_call" | custom-call | tf_op jit(solution)/shard_map/wave_sum/pallas_call | solution.py:167
  97.9 0.8 slice.1329
  98.8 0.9 subtract_divide_fusion.1
  99.8 0.3 multiply_subtract_fusion
  100.2 2.4 %copy.475 = f32[8,2,50,500]{3,1,2,0:T(2,128)} copy(f32[8,2,50,500]{3,0,2,1:T(8,128)S(1)} %multiply_subtract_fusion) | data formatting | bytes 3200000
  (97 shorter events, 1.1 us)
Async XLA Ops:
  0.6 3.1 %copy-start.11 = (s32[8,2,50,500]{3,1,2,0:T(2,128)S(1)}, s32[8,2,50,500]{3,1,2,0:T(2,128)}, u32[]{:S(2)}) copy-start(s32[8,2,50,500]{3,1,2,0:T(2,128)} %param.10) | copy-start | bytes 4800004
  0.6 3.1 %copy-start.12 = (f32[8,2,50,500]{3,1,2,0:T(2,128)S(1)}, f32[8,2,50,500]{3,1,2,0:T(2,128)}, u32[]{:S(2)}) copy-start(f32[8,2,50,500]{3,1,2,0:T(2,128)} %param.8) | copy-start | bytes 4800004
  0.7 3.4 %copy-start.10 = (f32[8,2,50,500]{3,1,2,0:T(2,128)S(1)}, f32[8,2,50,500]{3,1,2,0:T(2,128)}, u32[]{:S(2)}) copy-start(f32[8,2,50,500]{3,1,2,0:T(2,128)} %param.9) | copy-start | bytes 4800004
  5.6 1.5 %copy-start.8 = (f32[1,8,2,50,500]{4,1,3,2,0:T(8,128)}, f32[1,8,2,50,500]{4,1,3,2,0:T(8,128)S(1)}, u32[]{:S(2)}) copy-start(f32[1,8,2,50,500]{4,1,3,2,0:T(8,128)S(1)} %get-tuple-element.435) | copy-start | bytes 4800004
  5.6 2.1 %copy-start.9 = (f32[1,8,2,50,500]{4,1,3,2,0:T(8,128)}, f32[1,8,2,50,500]{4,1,3,2,0:T(8,128)S(1)}, u32[]{:S(2)}) copy-start(f32[1,8,2,50,500]{4,1,3,2,0:T(8,128)S(1)} %get-tuple-element.436) | copy-start | bytes 4800004
  5.6 9.3 %copy-start.15 = (s32[2,40]{1,0:T(2,128)S(1)}, s32[2,40]{1,0:T(2,128)}, u32[]{:S(2)}) copy-start(s32[2,40]{1,0:T(2,128)} %param.13) | copy-start | bytes 964
  7.7 11.4 %collective-permute-start = (f32[4,8,2,4,500]{4,1,3,2,0:T(8,128)}, f32[4,8,2,4,500]{4,1,3,2,0:T(8,128)}, u32[]{:S(2)}, u32[]{:S(2)}) collective-permute-start(f32[4,8,2,4,500]{4,1,3,2,0:T(8,128)} %get-tuple-element.417), channel_id=1, source_target_pairs={{0,1},{1,2},{2,3},{3,4},{4,5},{5,6},{6,7},{7,8},{8,9},{9,10},{10,1... | collective-permute-start | bytes 1536008 | tf_op jit(solution)/shard_map/ppermute | solution.py:25
  12.6 10.8 %collective-permute-start.1 = (f32[4,8,2,4,500]{4,1,3,2,0:T(8,128)}, f32[4,8,2,4,500]{4,1,3,2,0:T(8,128)}, u32[]{:S(2)}, u32[]{:S(2)}) collective-permute-start(f32[4,8,2,4,500]{4,1,3,2,0:T(8,128)} %get-tuple-element.418), channel_id=1, source_target_pairs={{1,0},{2,1},{3,2},{4,3},{5,4},{6,5},{7,6},{8,7},{9,8},{10,9},{11,1... | collective-permute-start | bytes 1536008 | tf_op jit(solution)/shard_map/ppermute | solution.py:27
  28.3 7.7 %copy-start.2 = (f32[58,8,2,500]{3,1,2,0:T(8,128)}, f32[58,8,2,500]{3,1,2,0:T(8,128)S(1)}, u32[]{:S(2)}) copy-start(f32[58,8,2,500]{3,1,2,0:T(8,128)S(1)} %get-tuple-element.409) | copy-start | bytes 5568004
  30.1 4.4 %copy-start.6 = (f32[58,8,2,500]{3,1,2,0:T(8,128)}, f32[58,8,2,500]{3,1,2,0:T(8,128)S(1)}, u32[]{:S(2)}) copy-start(f32[58,8,2,500]{3,1,2,0:T(8,128)S(1)} %get-tuple-element.411) | copy-start | bytes 5568004
  32.4 2.1 %copy-start.4 = (f32[58,8,2,500]{3,1,2,0:T(8,128)}, f32[58,8,2,500]{3,1,2,0:T(8,128)S(1)}, u32[]{:S(2)}) copy-start(f32[58,8,2,500]{3,1,2,0:T(8,128)S(1)} %get-tuple-element.420) | copy-start | bytes 5568004
  32.9 1.6 %copy-start = (f32[58,8,2,500]{3,1,0,2:T(8,128)}, f32[58,8,2,500]{3,1,0,2:T(8,128)S(1)}, u32[]{:S(2)}) copy-start(f32[58,8,2,500]{3,1,0,2:T(8,128)S(1)} %fusion) | copy-start | bytes 5568004
  37.7 9.8 %copy-start.7 = (f32[58,8,2,500]{3,1,2,0:T(8,128)S(1)}, f32[58,8,2,500]{3,1,2,0:T(8,128)}, u32[]{:S(2)}) copy-start(f32[58,8,2,500]{3,1,2,0:T(8,128)} %copy-done.6) | copy-start | bytes 5568004
  40.9 6.6 %copy-start.3 = (f32[58,8,2,500]{3,1,2,0:T(8,128)S(1)}, f32[58,8,2,500]{3,1,2,0:T(8,128)}, u32[]{:S(2)}) copy-start(f32[58,8,2,500]{3,1,2,0:T(8,128)} %copy-done.2) | copy-start | bytes 5568004
  43.1 4.4 %copy-start.1 = (f32[58,8,2,500]{3,1,0,2:T(8,128)S(1)}, f32[58,8,2,500]{3,1,0,2:T(8,128)}, u32[]{:S(2)}) copy-start(f32[58,8,2,500]{3,1,0,2:T(8,128)} %copy-done) | copy-start | bytes 5568004
  45.3 2.4 %copy-start.5 = (f32[58,8,2,500]{3,1,2,0:T(8,128)S(1)}, f32[58,8,2,500]{3,1,2,0:T(8,128)}, u32[]{:S(2)}) copy-start(f32[58,8,2,500]{3,1,2,0:T(8,128)} %copy-done.4) | copy-start | bytes 5568004
  70.4 2.8 %copy-start.13 = (f32[2,8,50]{2,1,0:T(8,128)S(1)}, f32[2,8,50]{2,1,0:T(8,128)}, u32[]{:S(2)}) copy-start(f32[2,8,50]{2,1,0:T(8,128)} %spec_sum.1) | copy-start | bytes 9604
  98.8 1.4 %copy-start.14 = (f32[8,50]{1,0:T(8,128)}, f32[8,50]{1,0:T(8,128)S(1)}, u32[]{:S(2)}) copy-start(f32[8,50]{1,0:T(8,128)S(1)} %fusion.596) | copy-start | bytes 4804

commit v2 on v0

v2 whole, which is shorter than its diff:
```python
import jax
import jax.numpy as jnp
from jax import lax
from jax.experimental import pallas as pl
from jax.experimental.pallas import tpu as pltpu
from jax.sharding import PartitionSpec as P

F = 500
WIDE = 512
EXPO = 8
PAIR = 2
ROWS = 50
EDGE = 4
REG = 0.05
RIDGE = 1.0
MESH = pl.DeviceIdType.MESH

LINE = 8
CORES = 2
PLANE = 8
GROUP = 4
PARTS = 6
LOAD = 2 * WIDE + 128
FAR_FIRST = (4, 3, 5, 2, 6, 1, 7)

f32 = jnp.float32


def absorb(front, weight, outer, inner, pixel):
    a, b, d, ra, rb = front
    w_outer, w_inner, w_pixel = weight * outer, weight * inner, weight * pixel
    outer_square, inner_square = w_outer * outer, w_inner * inner
    a = a + outer_square + REG
    b = b + w_outer
    far = w_outer * inner
    d = d + weight
    ra = ra + outer * w_pixel
    rb = rb + w_pixel
    inverse = 1.0 / a
    near_factor, far_factor, start = b * inverse, far * inverse, ra * inverse
    front = (
        d - near_factor * b,
        w_inner - near_factor * far,
        inner_square - far_factor * far,
        rb - b * start,
        inner * w_pixel - far * start,
    )
    return front, (near_factor, far_factor, start), outer_square, inner_square


def main_kernel(
    px_hbm, iv_hbm, mk_hbm, lf_hbm, rt_hbm, sky_ref,
    flux, slope_ref, model_ref,
    px, iv, mk, lf, rt, near, far, start, prec,
    out_edge, in_edge, sums, boxes, model_s, load, box_a, part, box_b, piece,
    load_sem, edge_send, edge_recv, spec_send, spec_recv, smem_sem,
    a_send, a_recv, b_send, b_recv, c_send, c_recv,
):
    me = lax.axis_index("wave")
    count = lax.axis_size("wave")
    spec = lax.axis_index("spec")
    specs = lax.axis_size("spec")
    core = lax.rem(me, CORES)
    col = lax.rem(lax.div(me, CORES), LINE)
    row = lax.div(me, CORES * LINE)
    mem = row * CORES + core

    def plane_peer(d):
        other = lax.rem(mem + d, PLANE)
        return other, (lax.div(other, CORES) * LINE + col) * CORES + lax.rem(other, CORES)

    def line_peer(d):
        return (row * LINE + lax.rem(col + d, LINE)) * CORES + core

    following = lax.rem(me + 1, count)
    preceding = lax.rem(me + count - 1, count)

    def send(src, dst, send_sem, recv_sem, where):
        return pltpu.make_async_remote_copy(
            src_ref=src, dst_ref=dst, send_sem=send_sem, recv_sem=recv_sem, device_id=where, device_id_type=MESH
        )

    hbm = (iv_hbm, mk_hbm, lf_hbm, rt_hbm, px_hbm)
    vmem = (iv, mk, lf, rt, px)
    spans = (pl.ds(ROWS - EDGE, EDGE), pl.ds(0, EDGE), pl.ds(EDGE, ROWS - 2 * EDGE))
    loads = [
        [pltpu.make_async_copy(h.at[:, span], v.at[:, span], load_sem.at[i, j]) for j, (h, v) in enumerate(zip(hbm, vmem))]
        for i, span in enumerate(spans)
    ]
    for group in loads:
        for copy in group:
            copy.start()

    barrier = pltpu.get_barrier_semaphore()
    peers = [{"wave": following}, {"wave": preceding}]
    peers += [{"spec": lax.rem(spec + d, specs)} for d in range(1, specs)]
    peers += [{"wave": line_peer(d)} for d in FAR_FIRST]
    peers += [{"wave": plane_peer(d)[1]} for d in FAR_FIRST]
    for peer in peers:
        pl.semaphore_signal(barrier, inc=1, device_id=peer, device_id_type=MESH)

    def weight_of(es, n):
        return iv[es, n] * (1.0 - mk[es, n].astype(f32))

    def reduce_edge(side, rows, outer, inner):
        for g in range(EXPO // GROUP):
            es = pl.ds(g * GROUP, GROUP)
            first = rows[0]
            weight = weight_of(es, first)
            w_inner, w_pixel = weight * inner[es, first], weight * px[es, first]
            front = (weight, w_inner, w_inner * inner[es, first], w_pixel, inner[es, first] * w_pixel)
            inner_square = None
            for n in rows[1:]:
                front, _, _, inner_square = absorb(front, weight_of(es, n), outer[es, n], inner[es, n], px[es, n])
            for i, value in enumerate(front + (inner_square,)):
                out_edge[side, g, i] = value

    for copy in loads[0]:
        copy.wait()
    reduce_edge(0, tuple(range(ROWS - EDGE, ROWS)), lf, rt)
    for copy in loads[1]:
        copy.wait()
    reduce_edge(1, tuple(range(EDGE - 1, -1, -1)), rt, lf)

    pl.semaphore_wait(barrier, len(peers))
    edges = []
    for g in range(EXPO // GROUP):
        for side, where in ((0, following), (1, preceding)):
            copy = send(
                out_edge.at[side, g], in_edge.at[side, g], edge_send.at[side, g], edge_recv.at[side, g], {"wave": where}
            )
            copy.start()
            edges.append(copy)
    for copy in loads[2]:
        copy.wait()

    no_before = me == 0
    no_after = me == count - 1
    for g in range(EXPO // GROUP):
        es = pl.ds(g * GROUP, GROUP)
        edges[2 * g].wait_recv()
        a, b, d, ra, rb, last_square = (jnp.where(no_before, 0.0, in_edge[0, g, i]) for i in range(PARTS))

        def forward(n, carry, es=es):
            front, partial, last_square = carry
            weight = weight_of(es, n)
            front, factors, outer_square, inner_square = absorb(front, weight, lf[es, n], rt[es, n], px[es, n])
            prec[es, n] = partial + outer_square
            near[es, n], far[es, n], start[es, n] = factors
            return front, weight + last_square + REG, inner_square

        front, partial, _ = lax.fori_loop(
            0, ROWS, forward, ((a, b, d, ra, rb), jnp.zeros_like(a), last_square), unroll=5
        )
        edges[2 * g + 1].wait_recv()
        a2, b2, d2, ra2, rb2, next_square = (jnp.where(no_after, 0.0, in_edge[1, g, i]) for i in range(PARTS))
        a, b, d, ra, rb = front
        prec[es, ROWS] = partial + next_square
        b = b + b2
        inverse = 1.0 / (a + d2 + REG)
        factor, base = b * inverse, (ra + rb2) * inverse
        beyond = (rb + ra2 - b * base) / (d + a2 + REG - factor * b)
        edge_flux = base - factor * beyond
        flux[es, ROWS - 1] = edge_flux

        def backward(i, carry, es=es):
            next_one, next_two = carry
            n = ROWS - 1 - i
            value = start[es, n] - near[es, n] * next_one - far[es, n] * next_two
            flux[es, n - 1] = value
            return value, next_one

        lax.fori_loop(0, ROWS - 1, backward, (edge_flux, beyond), unroll=7)

    is_sky = sky_ref[...][None]
    lane16 = lax.broadcasted_iota(jnp.int32, (EXPO * PAIR, 128), 1)

    def fold(value):
        return jnp.sum(value.reshape(EXPO * PAIR, F), axis=1, keepdims=True)

    def sky_row(n, carry):
        top, bottom = carry
        share = prec[:, n + 1] * is_sky
        scaled = share * flux[:, n]
        return jnp.where(lane16 == n, fold(scaled), top), jnp.where(lane16 == n, fold(share), bottom)

    zero16 = jnp.zeros((EXPO * PAIR, 128), f32)
    top, bottom = lax.fori_loop(0, ROWS, sky_row, (zero16, zero16), unroll=10)
    sums[0] = top.reshape(EXPO, PAIR, 128).sum(1)
    sums[1] = bottom.reshape(EXPO, PAIR, 128).sum(1)
    sky_copies = []
    for d in range(1, specs):
        copy = send(
            sums, boxes.at[specs - 1 - d], spec_send.at[d - 1], spec_recv.at[specs - 1 - d], {"spec": lax.rem(spec + d, specs)}
        )
        copy.start()
        sky_copies.append(copy)
    for copy in sky_copies:
        copy.wait_recv()
    held = [sums[...]] + [boxes[k] for k in range(specs - 1)]
    total = None
    for s in range(specs):
        place = lax.rem(s - spec + specs, specs)
        term = held[0]
        for k in range(1, specs):
            term = jnp.where(place == k, held[k], term)
        total = term if total is None else total + term
    lane = lax.broadcasted_iota(jnp.int32, (EXPO, 128), 1)
    used = lane < ROWS
    model_ref[...] = jnp.where(used, total[0], 0.0) / jnp.where(used, total[1], 1.0)
    to_scalar = pltpu.make_async_copy(model_ref, model_s, smem_sem)
    to_scalar.start()
    to_scalar.wait()

    scale = 2.0 / (count * ROWS - 1)
    base_row = me * ROWS
    lane2 = lax.broadcasted_iota(jnp.int32, (PAIR, 128), 1)

    def regress(n, carry):
        first, second, moment = carry
        place = (base_row + n).astype(f32) * scale - 1.0
        powers = jnp.where(lane2 == 0, 1.0, jnp.where(lane2 == 1, place, place * place))
        first, second, moment = list(first), list(second), list(moment)
        for e in range(EXPO):
            sky = model_s[e, n]
            term = flux[e, n] * sky
            first[e] = first[e] + term
            second[e] = second[e] + term * place
            moment[e] = moment[e] + powers * (sky * sky)
        return tuple(first), tuple(second), tuple(moment)

    zero = jnp.zeros((PAIR, F), f32)
    first, second, moment = lax.fori_loop(
        0, ROWS, regress, ((zero,) * EXPO, (zero,) * EXPO, (jnp.zeros((PAIR, 128), f32),) * EXPO), unroll=2
    )
    for e in range(EXPO):
        load[e, :, 0:F] = first[e]
        load[e, :, WIDE : WIDE + F] = second[e]
        load[e, :, 2 * WIDE : LOAD] = moment[e]

    for d in FAR_FIRST:
        other, where = plane_peer(d)
        send(load.at[other], box_a.at[PLANE - 1 - d], a_send, a_recv, {"wave": where}).start()
    whole_a = send(box_a, box_a, a_send, a_recv, {"wave": following})
    whole_a.wait_recv()
    acc = load[mem]
    for k in range(PLANE - 1):
        acc = acc + box_a[k]
    part[...] = acc
    for d in FAR_FIRST:
        send(part, box_b.at[LINE - 1 - d], b_send, b_recv, {"wave": line_peer(d)}).start()
    whole_b = send(box_b, box_b, b_send, b_recv, {"wave": following})
    whole_b.wait_recv()
    for k in range(LINE - 1):
        acc = acc + box_b[k]
    first_sum, second_sum, powers_sum = acc[:, :WIDE], acc[:, WIDE : 2 * WIDE], acc[:, 2 * WIDE : LOAD]

    def pick(i):
        return jnp.sum(jnp.where(lane2 == i, powers_sum, 0.0), axis=1, keepdims=True)

    upper, cross, lower = pick(0) + RIDGE, pick(1), pick(2) + RIDGE
    inverse = 1.0 / (upper * lower - cross * cross)
    piece[0] = (lower * first_sum - cross * second_sum) * inverse
    piece[1] = (upper * second_sum - cross * first_sum) * inverse
    slope_ref[mem] = piece[...]
    for d in FAR_FIRST:
        send(piece, slope_ref.at[mem], c_send, c_recv, {"wave": plane_peer(d)[1]}).start()
    whole_c = send(slope_ref.at[pl.ds(0, PLANE - 1)], slope_ref.at[pl.ds(0, PLANE - 1)], c_send, c_recv, {"wave": following})
    whole_c.wait_recv()
    for copy in edges + sky_copies:
        copy.wait_send()
    whole_a.wait_send()
    whole_b.wait_send()
    whole_c.wait_send()


def local(pixels, ivar, mask, psf_left, psf_right, sky_index):
    is_sky = jnp.sum((sky_index[:, :, None] == jnp.arange(F)[None, None, :]).astype(f32), axis=1)
    turned = [jnp.transpose(v, (0, 2, 1, 3)) for v in (pixels, ivar, mask, psf_left, psf_right)]
    field = (EXPO, ROWS, PAIR, F)
    specs = lax.axis_size("spec")
    hbm, vmem = pl.BlockSpec(memory_space=pltpu.HBM), pl.BlockSpec(memory_space=pltpu.VMEM)
    dma = pltpu.SemaphoreType.DMA
    groups = EXPO // GROUP
    edge = (2, groups, PARTS, GROUP, PAIR, F)
    flux, slopes, model = pl.pallas_call(
        main_kernel,
        out_shape=(
            jax.ShapeDtypeStruct(field, f32),
            jax.ShapeDtypeStruct((EXPO, 2, PAIR, WIDE), f32),
            jax.ShapeDtypeStruct((EXPO, 128), f32),
        ),
        in_specs=[hbm] * 5 + [vmem],
        out_specs=(vmem, vmem, vmem),
        scratch_shapes=[
            pltpu.VMEM(field, f32),
            pltpu.VMEM(field, f32),
            pltpu.VMEM(field, jnp.int32),
            pltpu.VMEM(field, f32),
            pltpu.VMEM(field, f32),
            pltpu.VMEM(field, f32),
            pltpu.VMEM(field, f32),
            pltpu.VMEM(field, f32),
            pltpu.VMEM((EXPO, ROWS + 1, PAIR, F), f32),
            pltpu.VMEM(edge, f32),
            pltpu.VMEM(edge, f32),
            pltpu.VMEM((2, EXPO, 128), f32),
            pltpu.VMEM((specs - 1, 2, EXPO, 128), f32),
            pltpu.SMEM((EXPO, 128), f32),
            pltpu.VMEM((EXPO, PAIR, LOAD), f32),
            pltpu.VMEM((PLANE - 1, PAIR, LOAD), f32),
            pltpu.VMEM((PAIR, LOAD), f32),
            pltpu.VMEM((LINE - 1, PAIR, LOAD), f32),
            pltpu.VMEM((2, PAIR, WIDE), f32),
            dma((3, 5)),
            dma((2, groups)),
            dma((2, groups)),
            dma((specs - 1,)),
            dma((specs - 1,)),
            dma,
            dma,
            dma,
            dma,
            dma,
            dma,
            dma,
        ],
        compiler_params=pltpu.CompilerParams(
            collective_id=0, has_side_effects=True, vmem_limit_bytes=40 * 1024 * 1024
        ),
        name="deconvolve",
    )(*turned, is_sky)
    model = model[:, :ROWS]
    total_rows = ROWS * lax.axis_size("wave")
    offsets = lax.axis_index("wave") * ROWS + jnp.arange(ROWS)
    position = 2.0 * offsets.astype(f32) / (total_rows - 1) - 1.0
    slope_a, slope_b = slopes[:, None, 0, :, :F], slopes[:, None, 1, :, :F]
    fitted = (slope_a + slope_b * position[None, :, None, None]) * model[:, :, None, None]
    return (jnp.transpose(flux - fitted, (0, 2, 1, 3)), model)


def solution(mesh):
    in_specs = (
        P(None, "spec", "wave", None),
        P(None, "spec", "wave", None),
        P(None, "spec", "wave", None),
        P(None, "spec", "wave", None),
        P(None, "spec", "wave", None),
        P("spec", None),
    )
    out_specs = (P(None, "spec", "wave", None), P(None, "wave"))
    return jax.shard_map(local, mesh=mesh, in_specs=in_specs, out_specs=out_specs, check_vma=False)
```

time: 327 us -> 46.5 us (0.14)
  blocking collectives: 253 us -> 0 us
  Pallas kernels: 0 us -> 34.9 us
  other arithmetic: 34.4 us -> 2.98 us
  matrix products: 10.7 us -> 0 us
  waiting for transfers between devices: 8.39 us -> 0 us
  starting transfers between devices: 7.21 us -> 0 us
    psum x2 -> x0, blocking collectives: 253 us -> none  [the longest x1 244 us: local(): moments, fibre_sums = lax.psum((moments, fibre_sums), 'wave')]
    pallas_call x0 -> x1, Pallas kernels: none -> 34.9 us  [local(): pl.pallas_call(main_kernel, out_shape=(jax.ShapeDtypeStruct(field, f32),...]
    div x33 -> x0, other arithmetic: 22.4 us -> none  [the longest x12 10.9 us: band_substitute(): (rhs_rows[step_row] - lowers[step_row] * forward_last - farther[step_row]...]
    dot_general x4 -> x0, matrix products: 10.7 us -> none  [the longest x1 3.31 us: local(): jnp.einsum('eswf,sf->ew', precision, is_sky, precision=lax.Precision.HIGH...]
    ppermute x2 -> x0, waiting for transfers between devices: 8.39 us -> none  [the longest x1 4.4 us: extended_2(): lax.ppermute(head, axis, [((i + 1) % count, i) for i in range(ends)])]
    ppermute x2 -> x0, starting transfers between devices: 7.21 us -> none  [the longest x1 4.93 us: extended_2(): lax.ppermute(tail, axis, [(i, (i + 1) % count) for i in range(ends)])]
    unnamed x80 -> x11, local copies, waits for them, and re-layouts: 4.58 us -> 7.74 us
  transfers between devices with their start and end apart: 2 -> 0, of which waited for: 2 -> 0; matrix products, arithmetic and copies ran while one was open for 0% -> 0% of each run, Pallas kernels for 0% -> 0%
where the time goes in v2:
time: 46.5 us; the launch traced here: 46.3 us
  Pallas kernels  34.9 us (75%)
  local copies, waits for them, and re-layouts  7.74 us (17%)
  other arithmetic  2.98 us (6%)
  between operations  0.67 us (1%)
    pallas_call x1, Pallas kernels, local(): pl.pallas_call(main_kernel, out_shape=(jax.ShapeDtypeStruct(field, f32),...  34.9 us
    unnamed x11, local copies, waits for them, and re-layouts  7.74 us
    transpose x1, other arithmetic, local(): return (jnp.transpose(flux - fitted, (0, 2, 1, 3)), model)  2.2 us

profile of v2, /device:TPU:1, one launch (start us, length us, event | category | flops | bytes accessed | tf_op | source)
XLA Modules:
  0.0 46.3 jit_solution(2950955771029099138)
XLA Ops:
  0.6 0.8 %convert_reduce_fusion.sky_ref = f32[2,500]{1,0:T(2,128)S(1)} fusion(s32[2,40]{1,0:T(2,128)} %param.11), kind=kLoop, calls=%fused_computation.1 | loop fusion | flops 119000 | bytes 4320 | tf_op jit(solution)/shard_map/reduce_sum | solution.py:278
  1.4 0.0 copy-start
  1.4 1.4 %copy-done = f32[8,2,50,500]{3,1,2,0:T(2,128)S(1)} copy-done((f32[8,2,50,500]{3,1,2,0:T(2,128)S(1)}, f32[8,2,50,500]{3,1,2,0:T(2,128)}, u32[]{:S(2)}) %copy-start) | copy-done | bytes 1600024
  2.8 0.0 copy-start.1
  2.8 1.4 %copy-done.1 = f32[8,2,50,500]{3,1,2,0:T(2,128)S(1)} copy-done((f32[8,2,50,500]{3,1,2,0:T(2,128)S(1)}, f32[8,2,50,500]{3,1,2,0:T(2,128)}, u32[]{:S(2)}) %copy-start.1) | copy-done | bytes 1600024
  4.3 0.0 copy-start.2
  4.3 1.4 %copy-done.2 = s32[8,2,50,500]{3,1,2,0:T(2,128)S(1)} copy-done((s32[8,2,50,500]{3,1,2,0:T(2,128)S(1)}, s32[8,2,50,500]{3,1,2,0:T(2,128)}, u32[]{:S(2)}) %copy-start.2) | copy-done | bytes 1600024
  5.7 0.0 copy-start.3
  5.7 1.4 %copy-done.3 = f32[8,2,50,500]{3,1,2,0:T(2,128)S(1)} copy-done((f32[8,2,50,500]{3,1,2,0:T(2,128)S(1)}, f32[8,2,50,500]{3,1,2,0:T(2,128)}, u32[]{:S(2)}) %copy-start.3) | copy-done | bytes 1600024
  7.1 0.0 copy-start.4
  7.1 1.4 %copy-done.4 = f32[8,2,50,500]{3,1,2,0:T(2,128)S(1)} copy-done((f32[8,2,50,500]{3,1,2,0:T(2,128)S(1)}, f32[8,2,50,500]{3,1,2,0:T(2,128)}, u32[]{:S(2)}) %copy-start.4) | copy-done | bytes 1600024
  8.6 34.9 %deconvolve.1 = (f32[8,50,2,500]{3,2,1,0:T(2,128)S(1)}, f32[8,2,2,512]{3,2,1,0:T(2,128)S(1)}, f32[8,128]{1,0:T(8,128)S(1)}) custom-call(f32[8,50,2,500]{3,2,1,0:T(2,128)S(1)} %bitcast.12, f32[8,50,2,500]{3,2,1,0:T(2,128)S(1)} %bitcast.13, s32[8,50,2,500]{3,2,1,0:T(2,128)S(1)} %bitcast.14, f32[8,50,2,500]{3,2,1,0:T(2,128)S(1)} %bitcast.15, ...), custom_call_target="tpu_custom_call" | custom-call | tf_op jit(solution)/shard_map/deconvolve/pallas_call | solution.py:286
  43.5 2.2 %subtract_bitcast_fusion = f32[8,2,50,500]{3,1,2,0:T(2,128)} fusion(f32[8,50,2,500]{3,2,1,0:T(2,128)S(1)} %get-tuple-element.5, f32[8,50]{1,0:T(8,128)S(1)} %bitcast.17, f32[8,2,500]{2,1,0:T(2,128)S(1)} %get-tuple-element.9, f32[8,2,500]{2,1,0:T(2,128)S(1)} %get-tuple-element.8, f32[50]{0:T(128)S(1)} %multiply_add_fusion), kind=kLoop, calls=%fused_computation | loop fusion | flops 1600000 | bytes 3265800 | tf_op jit(solution)/shard_map/transpose | solution.py:339
  45.7 0.6 %copy.9 = f32[8,50]{1,0:T(8,128)} copy(f32[8,50]{1,0:T(8,128)S(1)} %bitcast.18) | data formatting | bytes 3200
  (2 shorter events, 0.0 us)
Async XLA Ops:
  1.4 1.4 %copy-start = (f32[8,2,50,500]{3,1,2,0:T(2,128)S(1)}, f32[8,2,50,500]{3,1,2,0:T(2,128)}, u32[]{:S(2)}) copy-start(f32[8,2,50,500]{3,1,2,0:T(2,128)} %param.6) | copy-start | bytes 4800004
  2.8 1.4 %copy-start.1 = (f32[8,2,50,500]{3,1,2,0:T(2,128)S(1)}, f32[8,2,50,500]{3,1,2,0:T(2,128)}, u32[]{:S(2)}) copy-start(f32[8,2,50,500]{3,1,2,0:T(2,128)} %param.7) | copy-start | bytes 4800004
  4.3 1.4 %copy-start.2 = (s32[8,2,50,500]{3,1,2,0:T(2,128)S(1)}, s32[8,2,50,500]{3,1,2,0:T(2,128)}, u32[]{:S(2)}) copy-start(s32[8,2,50,500]{3,1,2,0:T(2,128)} %param.8) | copy-start | bytes 4800004
  5.7 1.4 %copy-start.3 = (f32[8,2,50,500]{3,1,2,0:T(2,128)S(1)}, f32[8,2,50,500]{3,1,2,0:T(2,128)}, u32[]{:S(2)}) copy-start(f32[8,2,50,500]{3,1,2,0:T(2,128)} %param.9) | copy-start | bytes 4800004
  7.1 1.4 %copy-start.4 = (f32[8,2,50,500]{3,1,2,0:T(2,128)S(1)}, f32[8,2,50,500]{3,1,2,0:T(2,128)}, u32[]{:S(2)}) copy-start(f32[8,2,50,500]{3,1,2,0:T(2,128)} %param.10) | copy-start | bytes 4800004

commit v3 on v2

--- a/solution.py
+++ b/solution.py
@@ -49,11 +49,11 @@
 
 
 def main_kernel(
-    px_hbm, iv_hbm, mk_hbm, lf_hbm, rt_hbm, sky_ref,
-    flux, slope_ref, model_ref,
-    px, iv, mk, lf, rt, near, far, start, prec,
-    out_edge, in_edge, sums, boxes, model_s, load, box_a, part, box_b, piece,
-    load_sem, edge_send, edge_recv, spec_send, spec_recv, smem_sem,
+    px_hbm, iv_hbm, mk_hbm, lf_hbm, rt_hbm, index_hbm,
+    flux, model_ref,
+    px, iv, mk, lf, rt, index, near, far, start, prec,
+    out_edge, in_edge, sums, boxes, model_s, load, box_a, part, box_b, piece, slope_ref,
+    load_sem, index_sem, edge_send, edge_recv, spec_send, spec_recv, smem_sem,
     a_send, a_recv, b_send, b_recv, c_send, c_recv,
 ):
     me = lax.axis_index("wave")
@@ -90,6 +90,9 @@
     for group in loads:
         for copy in group:
             copy.start()
+
+    index_copy = pltpu.make_async_copy(index_hbm, index, index_sem)
+    index_copy.start()
 
     barrier = pltpu.get_barrier_semaphore()
     peers = [{"wave": following}, {"wave": preceding}]
@@ -131,6 +134,13 @@
             )
             copy.start()
             edges.append(copy)
+    fibre = lax.broadcasted_iota(jnp.int32, (PAIR, F), 1)
+    index_copy.wait()
+    listed = index[...]
+    is_sky = jnp.zeros((PAIR, F), f32)
+    for j in range(listed.shape[1]):
+        is_sky = is_sky + jnp.where(listed[:, j : j + 1] == fibre, 1.0, 0.0)
+    is_sky = is_sky[None]
     for copy in loads[2]:
         copy.wait()
 
@@ -172,7 +182,6 @@
 
         lax.fori_loop(0, ROWS - 1, backward, (edge_flux, beyond), unroll=7)
 
-    is_sky = sky_ref[...][None]
     lane16 = lax.broadcasted_iota(jnp.int32, (EXPO * PAIR, 128), 1)
 
     def fold(value):
@@ -267,6 +276,15 @@
         send(piece, slope_ref.at[mem], c_send, c_recv, {"wave": plane_peer(d)[1]}).start()
     whole_c = send(slope_ref.at[pl.ds(0, PLANE - 1)], slope_ref.at[pl.ds(0, PLANE - 1)], c_send, c_recv, {"wave": following})
     whole_c.wait_recv()
+
+    def clean(n, carry):
+        place = (base_row + n).astype(f32) * scale - 1.0
+        for e in range(EXPO):
+            fitted = slope_ref[e, 0, :, 0:F] + slope_ref[e, 1, :, 0:F] * place
+            flux[e, n] = flux[e, n] - fitted * model_s[e, n]
+        return carry
+
+    lax.fori_loop(0, ROWS, clean, 0, unroll=2)
     for copy in edges + sky_copies:
         copy.wait_send()
     whole_a.wait_send()
@@ -274,8 +292,17 @@
     whole_c.wait_send()
 
 
+def store_kernel(cleaned, model, cleaned_out, model_out, model_rows, sems):
+    main = pltpu.make_async_copy(cleaned, cleaned_out, sems.at[0])
+    main.start()
+    model_rows[...] = model[:, 0:ROWS]
+    small = pltpu.make_async_copy(model_rows, model_out, sems.at[1])
+    small.start()
+    small.wait()
+    main.wait()
+
+
 def local(pixels, ivar, mask, psf_left, psf_right, sky_index):
-    is_sky = jnp.sum((sky_index[:, :, None] == jnp.arange(F)[None, None, :]).astype(f32), axis=1)
     turned = [jnp.transpose(v, (0, 2, 1, 3)) for v in (pixels, ivar, mask, psf_left, psf_right)]
     field = (EXPO, ROWS, PAIR, F)
     specs = lax.axis_size("spec")
@@ -283,21 +310,21 @@
     dma = pltpu.SemaphoreType.DMA
     groups = EXPO // GROUP
     edge = (2, groups, PARTS, GROUP, PAIR, F)
-    flux, slopes, model = pl.pallas_call(
+    cleaned, model = pl.pallas_call(
         main_kernel,
         out_shape=(
             jax.ShapeDtypeStruct(field, f32),
-            jax.ShapeDtypeStruct((EXPO, 2, PAIR, WIDE), f32),
             jax.ShapeDtypeStruct((EXPO, 128), f32),
         ),
-        in_specs=[hbm] * 5 + [vmem],
-        out_specs=(vmem, vmem, vmem),
+        in_specs=[hbm] * 6,
+        out_specs=(vmem, vmem),
         scratch_shapes=[
             pltpu.VMEM(field, f32),
             pltpu.VMEM(field, f32),
             pltpu.VMEM(field, jnp.int32),
             pltpu.VMEM(field, f32),
             pltpu.VMEM(field, f32),
+            pltpu.VMEM(sky_index.shape, jnp.int32),
             pltpu.VMEM(field, f32),
             pltpu.VMEM(field, f32),
             pltpu.VMEM(field, f32),
@@ -312,7 +339,9 @@
             pltpu.VMEM((PAIR, LOAD), f32),
             pltpu.VMEM((LINE - 1, PAIR, LOAD), f32),
             pltpu.VMEM((2, PAIR, WIDE), f32),
+            pltpu.VMEM((EXPO, 2, PAIR, WIDE), f32),
             dma((3, 5)),
+            dma,
             dma((2, groups)),
             dma((2, groups)),
             dma((specs - 1,)),
@@ -326,17 +355,20 @@
             dma,
         ],
         compiler_params=pltpu.CompilerParams(
-            collective_id=0, has_side_effects=True, vmem_limit_bytes=40 * 1024 * 1024
+            collective_id=0, has_side_effects=True, vmem_limit_bytes=54_000_000
         ),
         name="deconvolve",
-    )(*turned, is_sky)
-    model = model[:, :ROWS]
-    total_rows = ROWS * lax.axis_size("wave")
-    offsets = lax.axis_index("wave") * ROWS + jnp.arange(ROWS)
-    position = 2.0 * offsets.astype(f32) / (total_rows - 1) - 1.0
-    slope_a, slope_b = slopes[:, None, 0, :, :F], slopes[:, None, 1, :, :F]
-    fitted = (slope_a + slope_b * position[None, :, None, None]) * model[:, :, None, None]
-    return (jnp.transpose(flux - fitted, (0, 2, 1, 3)), model)
+    )(*turned, sky_index)
+    cleaned, model = pl.pallas_call(
+        store_kernel,
+        out_shape=(jax.ShapeDtypeStruct(field, f32), jax.ShapeDtypeStruct((EXPO, ROWS), f32)),
+        in_specs=[vmem, vmem],
+        out_specs=(hbm, hbm),
+        scratch_shapes=[pltpu.VMEM((EXPO, ROWS), f32), dma((2,))],
+        compiler_params=pltpu.CompilerParams(vmem_limit_bytes=54_000_000),
+        name="store",
+    )(cleaned, model)
+    return (jnp.transpose(cleaned, (0, 2, 1, 3)), model)
 
 
 def solution(mesh):

time: 46.5 us -> 37.4 us (0.80)
  local copies, waits for them, and re-layouts: 7.74 us -> 0.67 us
  other arithmetic: 2.98 us -> 0 us
  Pallas kernels: 34.9 us -> 36 us
    unnamed x11 -> x2, local copies, waits for them, and re-layouts: 7.74 us -> 0.67 us
    transpose x1 -> x0, other arithmetic: 2.2 us -> none  [local(): return (jnp.transpose(flux - fitted, (0, 2, 1, 3)), model)]
    pallas_call x0 -> x1, Pallas kernels: none -> 1.18 us  [local(): pl.pallas_call(store_kernel, out_shape=(jax.ShapeDtypeStruct(field, f32),...]
    reduce_sum x1 -> x0, other arithmetic: 0.78 us -> none  [local(): jnp.sum((sky_index[:, :, None] == jnp.arange(F)[None, None, :]).astype(f3...]
where the time goes in v3:
time: 37.4 us; the launch traced here: 37.3 us
  Pallas kernels  36 us (96%)
  local copies, waits for them, and re-layouts  0.67 us (2%)
  between operations  0.65 us (2%)
    pallas_call x1, Pallas kernels, local(): pl.pallas_call(main_kernel, out_shape=(jax.ShapeDtypeStruct(field, f32),...  34.8 us
    pallas_call x1, Pallas kernels, local(): pl.pallas_call(store_kernel, out_shape=(jax.ShapeDtypeStruct(field, f32),...  1.18 us

profile of v3, /device:TPU:1, one launch (start us, length us, event | category | flops | bytes accessed | tf_op | source)
XLA Modules:
  0.0 37.3 jit_solution(15065695095917767980)
XLA Ops:
  0.6 0.0 copy-start
  0.6 0.7 %copy-done = s32[2,40]{1,0:T(2,128)S(1)} copy-done((s32[2,40]{1,0:T(2,128)S(1)}, s32[2,40]{1,0:T(2,128)}, u32[]{:S(2)}) %copy-start) | copy-done | bytes 344
  1.3 34.8 %deconvolve.1 = (f32[8,50,2,500]{3,2,1,0:T(2,128)S(1)}, f32[8,128]{1,0:T(8,128)S(1)}) custom-call(f32[8,50,2,500]{3,2,1,0:T(2,128)} %bitcast.6, f32[8,50,2,500]{3,2,1,0:T(2,128)} %bitcast.7, s32[8,50,2,500]{3,2,1,0:T(2,128)} %bitcast.8, f32[8,50,2,500]{3,2,1,0:T(2,128)} %bitcast.9, f32[8,50,2,500]{3,2,1,0:T(2,128)} %bitcast.10, s32[2,40]{1,0:T(2,128)S(1)} %copy-done), custom_call_target="tpu_custom_call" | custom-call | tf_op jit(solution)/shard_map/deconvolve/pallas_call | solution.py:313
  36.1 1.2 %store.1 = (f32[8,50,2,500]{3,2,1,0:T(2,128)}, f32[8,50]{1,0:T(8,128)}) custom-call(f32[8,50,2,500]{3,2,1,0:T(2,128)S(1)} %get-tuple-element.6.cleaned, f32[8,128]{1,0:T(8,128)S(1)} %get-tuple-element.7.model), custom_call_target="tpu_custom_call" | custom-call | tf_op jit(solution)/shard_map/store/pallas_call | solution.py:362
Async XLA Ops:
  0.6 0.7 %copy-start = (s32[2,40]{1,0:T(2,128)S(1)}, s32[2,40]{1,0:T(2,128)}, u32[]{:S(2)}) copy-start(s32[2,40]{1,0:T(2,128)} %index_hbm.1) | copy-start | bytes 964

commit v4 on v3

--- a/solution.py
+++ b/solution.py
@@ -49,11 +49,11 @@
 
 
 def main_kernel(
-    px_hbm, iv_hbm, mk_hbm, lf_hbm, rt_hbm, index_hbm,
+    px_hbm, iv_hbm, mk_hbm, lf_hbm, rt_hbm, index,
     flux, model_ref,
-    px, iv, mk, lf, rt, index, near, far, start, prec,
-    out_edge, in_edge, sums, boxes, model_s, load, box_a, part, box_b, piece, slope_ref,
-    load_sem, index_sem, edge_send, edge_recv, spec_send, spec_recv, smem_sem,
+    px, iv, mk, lf, rt, near, far, start, prec,
+    out_edge, in_edge, sums, boxes, model_v, model_s, load, box_a, part, box_b, piece, slope_ref,
+    load_sem, edge_send, edge_recv, spec_send, spec_recv, smem_sem,
     a_send, a_recv, b_send, b_recv, c_send, c_recv,
 ):
     me = lax.axis_index("wave")
@@ -87,20 +87,20 @@
         [pltpu.make_async_copy(h.at[:, span], v.at[:, span], load_sem.at[i, j]) for j, (h, v) in enumerate(zip(hbm, vmem))]
         for i, span in enumerate(spans)
     ]
-    for group in loads:
+    barrier = pltpu.get_barrier_semaphore()
+
+    def greet(peers):
+        for peer in peers:
+            pl.semaphore_signal(barrier, inc=1, device_id=peer, device_id_type=MESH)
+        return len(peers)
+
+    greeted = greet([{"wave": line_peer(d)} for d in FAR_FIRST])
+    for group in loads[:2]:
         for copy in group:
             copy.start()
-
-    index_copy = pltpu.make_async_copy(index_hbm, index, index_sem)
-    index_copy.start()
-
-    barrier = pltpu.get_barrier_semaphore()
-    peers = [{"wave": following}, {"wave": preceding}]
-    peers += [{"spec": lax.rem(spec + d, specs)} for d in range(1, specs)]
-    peers += [{"wave": line_peer(d)} for d in FAR_FIRST]
-    peers += [{"wave": plane_peer(d)[1]} for d in FAR_FIRST]
-    for peer in peers:
-        pl.semaphore_signal(barrier, inc=1, device_id=peer, device_id_type=MESH)
+    greeted += greet([{"wave": plane_peer(d)[1]} for d in FAR_FIRST])
+    greeted += greet([{"spec": lax.rem(spec + d, specs)} for d in range(1, specs)])
+    greeted += greet([{"wave": following}, {"wave": preceding}])
 
     def weight_of(es, n):
         return iv[es, n] * (1.0 - mk[es, n].astype(f32))
@@ -125,7 +125,7 @@
         copy.wait()
     reduce_edge(1, tuple(range(EDGE - 1, -1, -1)), rt, lf)
 
-    pl.semaphore_wait(barrier, len(peers))
+    pl.semaphore_wait(barrier, greeted)
     edges = []
     for g in range(EXPO // GROUP):
         for side, where in ((0, following), (1, preceding)):
@@ -134,18 +134,26 @@
             )
             copy.start()
             edges.append(copy)
+    for copy in loads[2]:
+        copy.start()
     fibre = lax.broadcasted_iota(jnp.int32, (PAIR, F), 1)
-    index_copy.wait()
-    listed = index[...]
+    second_row = lax.broadcasted_iota(jnp.int32, (PAIR, F), 0) == 1
     is_sky = jnp.zeros((PAIR, F), f32)
-    for j in range(listed.shape[1]):
-        is_sky = is_sky + jnp.where(listed[:, j : j + 1] == fibre, 1.0, 0.0)
+    for j in range(index.shape[1]):
+        is_sky = is_sky + jnp.where(fibre == jnp.where(second_row, index[1, j], index[0, j]), 1.0, 0.0)
     is_sky = is_sky[None]
     for copy in loads[2]:
         copy.wait()
 
     no_before = me == 0
     no_after = me == count - 1
+    lane8 = lax.broadcasted_iota(jnp.int32, (GROUP * PAIR, 128), 1)
+    zero8 = jnp.zeros((GROUP * PAIR, 128), f32)
+
+    def fold(value):
+        return jnp.sum(value.reshape(GROUP * PAIR, F), axis=1, keepdims=True)
+
+    sky_copies = []
     for g in range(EXPO // GROUP):
         es = pl.ds(g * GROUP, GROUP)
         edges[2 * g].wait_recv()
@@ -182,74 +190,79 @@
 
         lax.fori_loop(0, ROWS - 1, backward, (edge_flux, beyond), unroll=7)
 
-    lane16 = lax.broadcasted_iota(jnp.int32, (EXPO * PAIR, 128), 1)
-
-    def fold(value):
-        return jnp.sum(value.reshape(EXPO * PAIR, F), axis=1, keepdims=True)
-
-    def sky_row(n, carry):
-        top, bottom = carry
-        share = prec[:, n + 1] * is_sky
-        scaled = share * flux[:, n]
-        return jnp.where(lane16 == n, fold(scaled), top), jnp.where(lane16 == n, fold(share), bottom)
-
-    zero16 = jnp.zeros((EXPO * PAIR, 128), f32)
-    top, bottom = lax.fori_loop(0, ROWS, sky_row, (zero16, zero16), unroll=10)
-    sums[0] = top.reshape(EXPO, PAIR, 128).sum(1)
-    sums[1] = bottom.reshape(EXPO, PAIR, 128).sum(1)
-    sky_copies = []
-    for d in range(1, specs):
-        copy = send(
-            sums, boxes.at[specs - 1 - d], spec_send.at[d - 1], spec_recv.at[specs - 1 - d], {"spec": lax.rem(spec + d, specs)}
+        def sky_row(n, carry, es=es):
+            top, bottom = carry
+            share = prec[es, n + 1] * is_sky
+            scaled = share * flux[es, n]
+            return jnp.where(lane8 == n, fold(scaled), top), jnp.where(lane8 == n, fold(share), bottom)
+
+        sums[g, 0], sums[g, 1] = lax.fori_loop(0, ROWS, sky_row, (zero8, zero8), unroll=10)
+        sky_copies.append(
+            [
+                send(
+                    sums.at[g], boxes.at[g, specs - 1 - d], spec_send.at[g, d - 1], spec_recv.at[g, specs - 1 - d],
+                    {"spec": lax.rem(spec + d, specs)},
+                )
+                for d in range(1, specs)
+            ]
         )
-        copy.start()
-        sky_copies.append(copy)
-    for copy in sky_copies:
-        copy.wait_recv()
-    held = [sums[...]] + [boxes[k] for k in range(specs - 1)]
-    total = None
-    for s in range(specs):
-        place = lax.rem(s - spec + specs, specs)
-        term = held[0]
-        for k in range(1, specs):
-            term = jnp.where(place == k, held[k], term)
-        total = term if total is None else total + term
-    lane = lax.broadcasted_iota(jnp.int32, (EXPO, 128), 1)
-    used = lane < ROWS
-    model_ref[...] = jnp.where(used, total[0], 0.0) / jnp.where(used, total[1], 1.0)
-    to_scalar = pltpu.make_async_copy(model_ref, model_s, smem_sem)
-    to_scalar.start()
-    to_scalar.wait()
+        for copy in sky_copies[g]:
+            copy.start()
 
     scale = 2.0 / (count * ROWS - 1)
     base_row = me * ROWS
     lane2 = lax.broadcasted_iota(jnp.int32, (PAIR, 128), 1)
-
-    def regress(n, carry):
-        first, second, moment = carry
-        place = (base_row + n).astype(f32) * scale - 1.0
-        powers = jnp.where(lane2 == 0, 1.0, jnp.where(lane2 == 1, place, place * place))
-        first, second, moment = list(first), list(second), list(moment)
-        for e in range(EXPO):
-            sky = model_s[e, n]
-            term = flux[e, n] * sky
-            first[e] = first[e] + term
-            second[e] = second[e] + term * place
-            moment[e] = moment[e] + powers * (sky * sky)
-        return tuple(first), tuple(second), tuple(moment)
-
+    used = lax.broadcasted_iota(jnp.int32, (GROUP, 128), 1) < ROWS
     zero = jnp.zeros((PAIR, F), f32)
-    first, second, moment = lax.fori_loop(
-        0, ROWS, regress, ((zero,) * EXPO, (zero,) * EXPO, (jnp.zeros((PAIR, 128), f32),) * EXPO), unroll=2
-    )
-    for e in range(EXPO):
-        load[e, :, 0:F] = first[e]
-        load[e, :, WIDE : WIDE + F] = second[e]
-        load[e, :, 2 * WIDE : LOAD] = moment[e]
-
-    for d in FAR_FIRST:
-        other, where = plane_peer(d)
-        send(load.at[other], box_a.at[PLANE - 1 - d], a_send, a_recv, {"wave": where}).start()
+    zero_moment = jnp.zeros((PAIR, 128), f32)
+    for g in range(EXPO // GROUP):
+        for copy in sky_copies[g]:
+            copy.wait_recv()
+        held = [sums[g]] + [boxes[g, k] for k in range(specs - 1)]
+        total = None
+        for s in range(specs):
+            place = lax.rem(s - spec + specs, specs)
+            term = held[0]
+            for k in range(1, specs):
+                term = jnp.where(place == k, held[k], term)
+            total = term if total is None else total + term
+        total = total.reshape(2, GROUP, PAIR, 128).sum(2)
+        model = jnp.where(used, total[0], 0.0) / jnp.where(used, total[1], 1.0)
+        model_v[g] = model
+        to_scalar = pltpu.make_async_copy(model_v.at[g], model_s.at[g], smem_sem)
+        to_scalar.start()
+        model_ref[g * GROUP : (g + 1) * GROUP] = model
+        to_scalar.wait()
+
+        def regress(n, carry, g=g):
+            first, second, moment = (list(v) for v in carry)
+            place = (base_row + n).astype(f32) * scale - 1.0
+            powers = jnp.where(lane2 == 0, 1.0, jnp.where(lane2 == 1, place, place * place))
+            for i in range(GROUP):
+                sky = model_s[g, i, n]
+                term = flux[g * GROUP + i, n] * sky
+                first[i] = first[i] + term
+                second[i] = second[i] + term * place
+                moment[i] = moment[i] + powers * (sky * sky)
+            return tuple(first), tuple(second), tuple(moment)
+
+        first, second, moment = lax.fori_loop(
+            0, ROWS, regress, ((zero,) * GROUP, (zero,) * GROUP, (zero_moment,) * GROUP), unroll=5
+        )
+        for i in range(GROUP):
+            e = g * GROUP + i
+            load[e, :, 0:F] = first[i]
+            load[e, :, WIDE : WIDE + F] = second[i]
+            load[e, :, 2 * WIDE : LOAD] = moment[i]
+        for i in range(GROUP):
+            e = g * GROUP + i
+            where = ((e // CORES) * LINE + col) * CORES + e % CORES
+            slot = lax.rem(mem - e + PLANE, PLANE) - 1
+
+            @pl.when(mem != e)
+            def _(e=e, where=where, slot=slot):
+                send(load.at[e], box_a.at[slot], a_send, a_recv, {"wave": where}).start()
+
     whole_a = send(box_a, box_a, a_send, a_recv, {"wave": following})
     whole_a.wait_recv()
     acc = load[mem]
@@ -277,15 +290,18 @@
     whole_c = send(slope_ref.at[pl.ds(0, PLANE - 1)], slope_ref.at[pl.ds(0, PLANE - 1)], c_send, c_recv, {"wave": following})
     whole_c.wait_recv()
 
+    slope_a = [slope_ref[e, 0, :, 0:F] for e in range(EXPO)]
+    slope_b = [slope_ref[e, 1, :, 0:F] for e in range(EXPO)]
+
     def clean(n, carry):
         place = (base_row + n).astype(f32) * scale - 1.0
         for e in range(EXPO):
-            fitted = slope_ref[e, 0, :, 0:F] + slope_ref[e, 1, :, 0:F] * place
-            flux[e, n] = flux[e, n] - fitted * model_s[e, n]
+            fitted = slope_a[e] + slope_b[e] * place
+            flux[e, n] = flux[e, n] - fitted * model_s[e // GROUP, e % GROUP, n]
         return carry
 
-    lax.fori_loop(0, ROWS, clean, 0, unroll=2)
-    for copy in edges + sky_copies:
+    lax.fori_loop(0, ROWS, clean, 0, unroll=5)
+    for copy in edges + sky_copies[0] + sky_copies[1]:
         copy.wait_send()
     whole_a.wait_send()
     whole_b.wait_send()
@@ -293,13 +309,14 @@
 
 
 def store_kernel(cleaned, model, cleaned_out, model_out, model_rows, sems):
-    main = pltpu.make_async_copy(cleaned, cleaned_out, sems.at[0])
-    main.start()
+    copies = [pltpu.make_async_copy(cleaned.at[e], cleaned_out.at[e], sems.at[e]) for e in range(EXPO)]
+    for copy in copies:
+        copy.start()
     model_rows[...] = model[:, 0:ROWS]
-    small = pltpu.make_async_copy(model_rows, model_out, sems.at[1])
-    small.start()
-    small.wait()
-    main.wait()
+    copies.append(pltpu.make_async_copy(model_rows, model_out, sems.at[EXPO]))
+    copies[-1].start()
+    for copy in copies:
+        copy.wait()
 
 
 def local(pixels, ivar, mask, psf_left, psf_right, sky_index):
@@ -316,7 +333,7 @@
             jax.ShapeDtypeStruct(field, f32),
             jax.ShapeDtypeStruct((EXPO, 128), f32),
         ),
-        in_specs=[hbm] * 6,
+        in_specs=[hbm] * 5 + [pl.BlockSpec(memory_space=pltpu.SMEM)],
         out_specs=(vmem, vmem),
         scratch_shapes=[
             pltpu.VMEM(field, f32),
@@ -324,16 +341,16 @@
             pltpu.VMEM(field, jnp.int32),
             pltpu.VMEM(field, f32),
             pltpu.VMEM(field, f32),
-            pltpu.VMEM(sky_index.shape, jnp.int32),
             pltpu.VMEM(field, f32),
             pltpu.VMEM(field, f32),
             pltpu.VMEM(field, f32),
             pltpu.VMEM((EXPO, ROWS + 1, PAIR, F), f32),
             pltpu.VMEM(edge, f32),
             pltpu.VMEM(edge, f32),
-            pltpu.VMEM((2, EXPO, 128), f32),
-            pltpu.VMEM((specs - 1, 2, EXPO, 128), f32),
-            pltpu.SMEM((EXPO, 128), f32),
+            pltpu.VMEM((groups, 2, GROUP * PAIR, 128), f32),
+            pltpu.VMEM((groups, specs - 1, 2, GROUP * PAIR, 128), f32),
+            pltpu.VMEM((groups, GROUP, 128), f32),
+            pltpu.SMEM((groups, GROUP, 128), f32),
             pltpu.VMEM((EXPO, PAIR, LOAD), f32),
             pltpu.VMEM((PLANE - 1, PAIR, LOAD), f32),
             pltpu.VMEM((PAIR, LOAD), f32),
@@ -341,11 +358,10 @@
             pltpu.VMEM((2, PAIR, WIDE), f32),
             pltpu.VMEM((EXPO, 2, PAIR, WIDE), f32),
             dma((3, 5)),
-            dma,
             dma((2, groups)),
             dma((2, groups)),
-            dma((specs - 1,)),
-            dma((specs - 1,)),
+            dma((groups, specs - 1)),
+            dma((groups, specs - 1)),
             dma,
             dma,
             dma,
@@ -364,7 +380,7 @@
         out_shape=(jax.ShapeDtypeStruct(field, f32), jax.ShapeDtypeStruct((EXPO, ROWS), f32)),
         in_specs=[vmem, vmem],
         out_specs=(hbm, hbm),
-        scratch_shapes=[pltpu.VMEM((EXPO, ROWS), f32), dma((2,))],
+        scratch_shapes=[pltpu.VMEM((EXPO, ROWS), f32), dma((EXPO + 1,))],
         compiler_params=pltpu.CompilerParams(vmem_limit_bytes=54_000_000),
         name="store",
     )(cleaned, model)

time: 37.4 us -> 37.7 us (level)
  no operation moved by 1% of the time
where the time goes in v4:
time: 37.7 us; the launch traced here: 37.6 us
  Pallas kernels  36.3 us (96%)
  local copies, waits for them, and re-layouts  0.67 us (2%)
  between operations  0.65 us (2%)
    pallas_call x1, Pallas kernels, local(): pl.pallas_call(main_kernel, out_shape=(jax.ShapeDtypeStruct(field, f32),...  35.1 us
    pallas_call x1, Pallas kernels, local(): pl.pallas_call(store_kernel, out_shape=(jax.ShapeDtypeStruct(field, f32),...  1.24 us

profile of v4, /device:TPU:1, one launch (start us, length us, event | category | flops | bytes accessed | tf_op | source)
XLA Modules:
  0.0 37.6 jit_solution(15051680229699153559)
XLA Ops:
  0.6 0.0 copy-start
  0.6 0.7 %copy-done = s32[2,40]{1,0:T(2,128)S(1)} copy-done((s32[2,40]{1,0:T(2,128)S(1)}, s32[2,40]{1,0:T(2,128)}, u32[]{:S(2)}) %copy-start) | copy-done | bytes 344
  1.3 35.1 %deconvolve.1 = (f32[8,50,2,500]{3,2,1,0:T(2,128)S(1)}, f32[8,128]{1,0:T(8,128)S(1)}) custom-call(f32[8,50,2,500]{3,2,1,0:T(2,128)} %bitcast.6, f32[8,50,2,500]{3,2,1,0:T(2,128)} %bitcast.7, s32[8,50,2,500]{3,2,1,0:T(2,128)} %bitcast.8, f32[8,50,2,500]{3,2,1,0:T(2,128)} %bitcast.9, f32[8,50,2,500]{3,2,1,0:T(2,128)} %bitcast.10, s32[2,40]{1,0:T(2,128)S(1)} %copy-done), custom_call_target="tpu_custom_call" | custom-call | tf_op jit(solution)/shard_map/deconvolve/pallas_call | solution.py:330
  36.4 1.2 %store.1 = (f32[8,50,2,500]{3,2,1,0:T(2,128)}, f32[8,50]{1,0:T(8,128)}) custom-call(f32[8,50,2,500]{3,2,1,0:T(2,128)S(1)} %get-tuple-element.6.cleaned, f32[8,128]{1,0:T(8,128)S(1)} %get-tuple-element.7.model), custom_call_target="tpu_custom_call" | custom-call | tf_op jit(solution)/shard_map/store/pallas_call | solution.py:378
Async XLA Ops:
  0.6 0.7 %copy-start = (s32[2,40]{1,0:T(2,128)S(1)}, s32[2,40]{1,0:T(2,128)}, u32[]{:S(2)}) copy-start(s32[2,40]{1,0:T(2,128)} %index.1) | copy-start | bytes 964

commit v5 on v4

--- a/solution.py
+++ b/solution.py
@@ -51,7 +51,7 @@
 def main_kernel(
     px_hbm, iv_hbm, mk_hbm, lf_hbm, rt_hbm, index,
     flux, model_ref,
-    px, iv, mk, lf, rt, near, far, start, prec,
+    px, iv, mk, lr, near, far, start, prec,
     out_edge, in_edge, sums, boxes, model_v, model_s, load, box_a, part, box_b, piece, slope_ref,
     load_sem, edge_send, edge_recv, spec_send, spec_recv, smem_sem,
     a_send, a_recv, b_send, b_recv, c_send, c_recv,
@@ -72,8 +72,8 @@
     def line_peer(d):
         return (row * LINE + lax.rem(col + d, LINE)) * CORES + core
 
-    following = lax.rem(me + 1, count)
-    preceding = lax.rem(me + count - 1, count)
+    partner = me + 1 - 2 * core
+    outside = lax.rem(me + 2 * core - 1 + count, count)
 
     def send(src, dst, send_sem, recv_sem, where):
         return pltpu.make_async_remote_copy(
@@ -81,7 +81,7 @@
         )
 
     hbm = (iv_hbm, mk_hbm, lf_hbm, rt_hbm, px_hbm)
-    vmem = (iv, mk, lf, rt, px)
+    vmem = (iv, mk, lr.at[0], lr.at[1], px)
     spans = (pl.ds(ROWS - EDGE, EDGE), pl.ds(0, EDGE), pl.ds(EDGE, ROWS - 2 * EDGE))
     loads = [
         [pltpu.make_async_copy(h.at[:, span], v.at[:, span], load_sem.at[i, j]) for j, (h, v) in enumerate(zip(hbm, vmem))]
@@ -100,42 +100,44 @@
             copy.start()
     greeted += greet([{"wave": plane_peer(d)[1]} for d in FAR_FIRST])
     greeted += greet([{"spec": lax.rem(spec + d, specs)} for d in range(1, specs)])
-    greeted += greet([{"wave": following}, {"wave": preceding}])
+    greeted += greet([{"wave": outside}, {"wave": partner}])
 
     def weight_of(es, n):
         return iv[es, n] * (1.0 - mk[es, n].astype(f32))
 
-    def reduce_edge(side, rows, outer, inner):
-        for g in range(EXPO // GROUP):
-            es = pl.ds(g * GROUP, GROUP)
-            first = rows[0]
-            weight = weight_of(es, first)
-            w_inner, w_pixel = weight * inner[es, first], weight * px[es, first]
-            front = (weight, w_inner, w_inner * inner[es, first], w_pixel, inner[es, first] * w_pixel)
-            inner_square = None
-            for n in rows[1:]:
-                front, _, _, inner_square = absorb(front, weight_of(es, n), outer[es, n], inner[es, n], px[es, n])
-            for i, value in enumerate(front + (inner_square,)):
-                out_edge[side, g, i] = value
-
-    for copy in loads[0]:
-        copy.wait()
-    reduce_edge(0, tuple(range(ROWS - EDGE, ROWS)), lf, rt)
-    for copy in loads[1]:
-        copy.wait()
-    reduce_edge(1, tuple(range(EDGE - 1, -1, -1)), rt, lf)
+    sides = ((46 - 43 * core, 1 - 2 * core, core, partner), (3 + 43 * core, 2 * core - 1, 1 - core, outside))
+
+    def reduce_edge(side, g):
+        base, step, outer, _ = sides[side]
+        es = pl.ds(g * GROUP, GROUP)
+        weight, inner = weight_of(es, base), lr[1 - outer, es, base]
+        w_inner, w_pixel = weight * inner, weight * px[es, base]
+        front = (weight, w_inner, w_inner * inner, w_pixel, inner * w_pixel)
+        for i in range(1, EDGE):
+            n = base + step * i
+            front, _, _, inner_square = absorb(front, weight_of(es, n), lr[outer, es, n], lr[1 - outer, es, n], px[es, n])
+        for i, value in enumerate(front + (inner_square,)):
+            out_edge[side, g, i] = value
+
+    for group in loads[:2]:
+        for copy in group:
+            copy.wait()
+    for copy in loads[2]:
+        copy.start()
+    for g in range(EXPO // GROUP):
+        for side in (1, 0):
+            reduce_edge(side, g)
 
     pl.semaphore_wait(barrier, greeted)
-    edges = []
+    edges = {}
     for g in range(EXPO // GROUP):
-        for side, where in ((0, following), (1, preceding)):
+        for side in (1, 0):
             copy = send(
-                out_edge.at[side, g], in_edge.at[side, g], edge_send.at[side, g], edge_recv.at[side, g], {"wave": where}
+                out_edge.at[side, g], in_edge.at[side, g], edge_send.at[side, g], edge_recv.at[side, g],
+                {"wave": sides[side][3]},
             )
             copy.start()
-            edges.append(copy)
-    for copy in loads[2]:
-        copy.start()
+            edges[side, g] = copy
     fibre = lax.broadcasted_iota(jnp.int32, (PAIR, F), 1)
     second_row = lax.broadcasted_iota(jnp.int32, (PAIR, F), 0) == 1
     is_sky = jnp.zeros((PAIR, F), f32)
@@ -145,54 +147,63 @@
     for copy in loads[2]:
         copy.wait()
 
-    no_before = me == 0
-    no_after = me == count - 1
     lane8 = lax.broadcasted_iota(jnp.int32, (GROUP * PAIR, 128), 1)
     zero8 = jnp.zeros((GROUP * PAIR, 128), f32)
 
     def fold(value):
         return jnp.sum(value.reshape(GROUP * PAIR, F), axis=1, keepdims=True)
 
+    first_row, row_step = (ROWS - 1) * (1 - core), 2 * core - 1
+    fronts = []
+    for g in range(EXPO // GROUP):
+        es = pl.ds(g * GROUP, GROUP)
+        edges[0, g].wait_recv()
+        a, b, d, ra, rb, last_square = (in_edge[0, g, i] for i in range(PARTS))
+
+        def forward(k, carry, es=es):
+            front, partial, last_square = carry
+            n = first_row + row_step * k
+            weight = weight_of(es, n)
+            front, factors, outer_square, inner_square = absorb(
+                front, weight, lr[1 - core, es, n], lr[core, es, n], px[es, n]
+            )
+            prec[es, k] = partial + outer_square
+            near[es, k], far[es, k], start[es, k] = factors
+            return front, weight + last_square + REG, inner_square
+
+        front, partial, _ = lax.fori_loop(
+            0, ROWS, forward, ((a, b, d, ra, rb), jnp.zeros_like(a), last_square), unroll=5
+        )
+        fronts.append((front, partial))
+
+    alone = (me == 0) | (me == count - 1)
     sky_copies = []
     for g in range(EXPO // GROUP):
         es = pl.ds(g * GROUP, GROUP)
-        edges[2 * g].wait_recv()
-        a, b, d, ra, rb, last_square = (jnp.where(no_before, 0.0, in_edge[0, g, i]) for i in range(PARTS))
-
-        def forward(n, carry, es=es):
-            front, partial, last_square = carry
-            weight = weight_of(es, n)
-            front, factors, outer_square, inner_square = absorb(front, weight, lf[es, n], rt[es, n], px[es, n])
-            prec[es, n] = partial + outer_square
-            near[es, n], far[es, n], start[es, n] = factors
-            return front, weight + last_square + REG, inner_square
-
-        front, partial, _ = lax.fori_loop(
-            0, ROWS, forward, ((a, b, d, ra, rb), jnp.zeros_like(a), last_square), unroll=5
-        )
-        edges[2 * g + 1].wait_recv()
-        a2, b2, d2, ra2, rb2, next_square = (jnp.where(no_after, 0.0, in_edge[1, g, i]) for i in range(PARTS))
-        a, b, d, ra, rb = front
+        edges[1, g].wait_recv()
+        a2, b2, d2, ra2, rb2, next_square = (jnp.where(alone, 0.0, in_edge[1, g, i]) for i in range(PARTS))
+        (a, b, d, ra, rb), partial = fronts[g]
         prec[es, ROWS] = partial + next_square
         b = b + b2
         inverse = 1.0 / (a + d2 + REG)
         factor, base = b * inverse, (ra + rb2) * inverse
         beyond = (rb + ra2 - b * base) / (d + a2 + REG - factor * b)
         edge_flux = base - factor * beyond
-        flux[es, ROWS - 1] = edge_flux
+        flux[es, first_row + row_step * (ROWS - 1)] = edge_flux
 
         def backward(i, carry, es=es):
             next_one, next_two = carry
-            n = ROWS - 1 - i
-            value = start[es, n] - near[es, n] * next_one - far[es, n] * next_two
-            flux[es, n - 1] = value
+            k = ROWS - 1 - i
+            value = start[es, k] - near[es, k] * next_one - far[es, k] * next_two
+            flux[es, first_row + row_step * (k - 1)] = value
             return value, next_one
 
         lax.fori_loop(0, ROWS - 1, backward, (edge_flux, beyond), unroll=7)
 
-        def sky_row(n, carry, es=es):
+        def sky_row(k, carry, es=es):
             top, bottom = carry
-            share = prec[es, n + 1] * is_sky
+            n = first_row + row_step * k
+            share = prec[es, k + 1] * is_sky
             scaled = share * flux[es, n]
             return jnp.where(lane8 == n, fold(scaled), top), jnp.where(lane8 == n, fold(share), bottom)
 
@@ -263,7 +274,7 @@
             def _(e=e, where=where, slot=slot):
                 send(load.at[e], box_a.at[slot], a_send, a_recv, {"wave": where}).start()
 
-    whole_a = send(box_a, box_a, a_send, a_recv, {"wave": following})
+    whole_a = send(box_a, box_a, a_send, a_recv, {"wave": partner})
     whole_a.wait_recv()
     acc = load[mem]
     for k in range(PLANE - 1):
@@ -271,7 +282,7 @@
     part[...] = acc
     for d in FAR_FIRST:
         send(part, box_b.at[LINE - 1 - d], b_send, b_recv, {"wave": line_peer(d)}).start()
-    whole_b = send(box_b, box_b, b_send, b_recv, {"wave": following})
+    whole_b = send(box_b, box_b, b_send, b_recv, {"wave": partner})
     whole_b.wait_recv()
     for k in range(LINE - 1):
         acc = acc + box_b[k]
@@ -287,7 +298,7 @@
     slope_ref[mem] = piece[...]
     for d in FAR_FIRST:
         send(piece, slope_ref.at[mem], c_send, c_recv, {"wave": plane_peer(d)[1]}).start()
-    whole_c = send(slope_ref.at[pl.ds(0, PLANE - 1)], slope_ref.at[pl.ds(0, PLANE - 1)], c_send, c_recv, {"wave": following})
+    whole_c = send(slope_ref.at[pl.ds(0, PLANE - 1)], slope_ref.at[pl.ds(0, PLANE - 1)], c_send, c_recv, {"wave": partner})
     whole_c.wait_recv()
 
     slope_a = [slope_ref[e, 0, :, 0:F] for e in range(EXPO)]
@@ -301,7 +312,7 @@
         return carry
 
     lax.fori_loop(0, ROWS, clean, 0, unroll=5)
-    for copy in edges + sky_copies[0] + sky_copies[1]:
+    for copy in list(edges.values()) + sky_copies[0] + sky_copies[1]:
         copy.wait_send()
     whole_a.wait_send()
     whole_b.wait_send()
@@ -339,8 +350,7 @@
             pltpu.VMEM(field, f32),
             pltpu.VMEM(field, f32),
             pltpu.VMEM(field, jnp.int32),
-            pltpu.VMEM(field, f32),
-            pltpu.VMEM(field, f32),
+            pltpu.VMEM((2,) + field, f32),
             pltpu.VMEM(field, f32),
             pltpu.VMEM(field, f32),
             pltpu.VMEM(field, f32),
@@ -374,7 +384,7 @@
             collective_id=0, has_side_effects=True, vmem_limit_bytes=54_000_000
         ),
         name="deconvolve",
-    )(*turned, sky_index)
+    )(*turned, pltpu.with_memory_space_constraint(sky_index, pltpu.HBM))
     cleaned, model = pl.pallas_call(
         store_kernel,
         out_shape=(jax.ShapeDtypeStruct(field, f32), jax.ShapeDtypeStruct((EXPO, ROWS), f32)),

time: 37.7 us -> 36.2 us (0.960)
  Pallas kernels: 36.3 us -> 35.5 us
  local copies, waits for them, and re-layouts: 0.67 us -> 0 us
    pallas_call x1, Pallas kernels: 35.1 us -> 34.2 us  [local(): pl.pallas_call(main_kernel, out_shape=(jax.ShapeDtypeStruct(field, f32),...]
    unnamed x2 -> x0, local copies, waits for them, and re-layouts: 0.67 us -> none
where the time goes in v5:
time: 36.2 us; the launch traced here: 36.1 us
  Pallas kernels  35.5 us (98%)
  between operations  0.64 us (2%)
    pallas_call x1, Pallas kernels, local(): pl.pallas_call(main_kernel, out_shape=(jax.ShapeDtypeStruct(field, f32),...  34.2 us
    pallas_call x1, Pallas kernels, local(): pl.pallas_call(store_kernel, out_shape=(jax.ShapeDtypeStruct(field, f32),...  1.24 us

profile of v5, /device:TPU:1, one launch (start us, length us, event | category | flops | bytes accessed | tf_op | source)
XLA Modules:
  0.0 36.1 jit_solution(11059892501406910742)
XLA Ops:
  0.6 34.2 %deconvolve.1 = (f32[8,50,2,500]{3,2,1,0:T(2,128)S(1)}, f32[8,128]{1,0:T(8,128)S(1)}) custom-call(f32[8,50,2,500]{3,2,1,0:T(2,128)} %bitcast.6, f32[8,50,2,500]{3,2,1,0:T(2,128)} %bitcast.7, s32[8,50,2,500]{3,2,1,0:T(2,128)} %bitcast.8, f32[8,50,2,500]{3,2,1,0:T(2,128)} %bitcast.9, f32[8,50,2,500]{3,2,1,0:T(2,128)} %bitcast.10, s32[2,40]{1,0:T(2,128)} %index.1), custom_call_target="tpu_custom_call" | custom-call | tf_op jit(solution)/shard_map/deconvolve/pallas_call | solution.py:341
  34.9 1.2 %store.1 = (f32[8,50,2,500]{3,2,1,0:T(2,128)}, f32[8,50]{1,0:T(8,128)}) custom-call(f32[8,50,2,500]{3,2,1,0:T(2,128)S(1)} %get-tuple-element.6.cleaned, f32[8,128]{1,0:T(8,128)S(1)} %get-tuple-element.7.model), custom_call_target="tpu_custom_call" | custom-call | tf_op jit(solution)/shard_map/store/pallas_call | solution.py:388

commit v6 on v5

--- a/solution.py
+++ b/solution.py
@@ -20,7 +20,10 @@
 PLANE = 8
 GROUP = 4
 PARTS = 6
-LOAD = 2 * WIDE + 128
+HALF = WIDE // 2
+LOAD = WIDE + 128
+LATE = 4
+SLICE = EXPO // LATE
 FAR_FIRST = (4, 3, 5, 2, 6, 1, 7)
 
 f32 = jnp.float32
@@ -52,8 +55,8 @@
     px_hbm, iv_hbm, mk_hbm, lf_hbm, rt_hbm, index,
     flux, model_ref,
     px, iv, mk, lr, near, far, start, prec,
-    out_edge, in_edge, sums, boxes, model_v, model_s, load, box_a, part, box_b, piece, slope_ref,
-    load_sem, edge_send, edge_recv, spec_send, spec_recv, smem_sem,
+    near_out, near_in, far_out, far_in, sums, boxes, model_v, model_s, load, box_a, part, box_b, piece, gathered, slope_ref,
+    load_sem, near_send, near_recv, far_send, far_recv, spec_send, spec_recv, smem_sem,
     a_send, a_recv, b_send, b_recv, c_send, c_recv,
 ):
     me = lax.axis_index("wave")
@@ -107,9 +110,9 @@
 
     sides = ((46 - 43 * core, 1 - 2 * core, core, partner), (3 + 43 * core, 2 * core - 1, 1 - core, outside))
 
-    def reduce_edge(side, g):
+    def reduce_edge(side, g, size, out):
         base, step, outer, _ = sides[side]
-        es = pl.ds(g * GROUP, GROUP)
+        es = pl.ds(g * size, size)
         weight, inner = weight_of(es, base), lr[1 - outer, es, base]
         w_inner, w_pixel = weight * inner, weight * px[es, base]
         front = (weight, w_inner, w_inner * inner, w_pixel, inner * w_pixel)
@@ -117,27 +120,31 @@
             n = base + step * i
             front, _, _, inner_square = absorb(front, weight_of(es, n), lr[outer, es, n], lr[1 - outer, es, n], px[es, n])
         for i, value in enumerate(front + (inner_square,)):
-            out_edge[side, g, i] = value
+            out[g, i] = value
 
     for group in loads[:2]:
         for copy in group:
             copy.wait()
     for copy in loads[2]:
         copy.start()
+    for g in range(LATE):
+        reduce_edge(1, g, SLICE, far_out)
     for g in range(EXPO // GROUP):
-        for side in (1, 0):
-            reduce_edge(side, g)
+        reduce_edge(0, g, GROUP, near_out)
 
     pl.semaphore_wait(barrier, greeted)
-    edges = {}
-    for g in range(EXPO // GROUP):
-        for side in (1, 0):
-            copy = send(
-                out_edge.at[side, g], in_edge.at[side, g], edge_send.at[side, g], edge_recv.at[side, g],
-                {"wave": sides[side][3]},
-            )
-            copy.start()
-            edges[side, g] = copy
+    far_edges = [
+        send(far_out.at[g], far_in.at[g], far_send.at[g], far_recv.at[g], {"wave": outside}) for g in range(LATE)
+    ]
+    near_edges = [
+        send(near_out.at[g], near_in.at[g], near_send.at[g], near_recv.at[g], {"wave": partner})
+        for g in range(EXPO // GROUP)
+    ]
+    far_edges[0].start()
+    for copy in near_edges:
+        copy.start()
+    for copy in far_edges[1:]:
+        copy.start()
     fibre = lax.broadcasted_iota(jnp.int32, (PAIR, F), 1)
     second_row = lax.broadcasted_iota(jnp.int32, (PAIR, F), 0) == 1
     is_sky = jnp.zeros((PAIR, F), f32)
@@ -147,18 +154,18 @@
     for copy in loads[2]:
         copy.wait()
 
-    lane8 = lax.broadcasted_iota(jnp.int32, (GROUP * PAIR, 128), 1)
-    zero8 = jnp.zeros((GROUP * PAIR, 128), f32)
+    lane4 = lax.broadcasted_iota(jnp.int32, (SLICE * PAIR, 128), 1)
+    zero4 = jnp.zeros((SLICE * PAIR, 128), f32)
 
     def fold(value):
-        return jnp.sum(value.reshape(GROUP * PAIR, F), axis=1, keepdims=True)
+        return jnp.sum(value.reshape(SLICE * PAIR, F), axis=1, keepdims=True)
 
     first_row, row_step = (ROWS - 1) * (1 - core), 2 * core - 1
     fronts = []
     for g in range(EXPO // GROUP):
         es = pl.ds(g * GROUP, GROUP)
-        edges[0, g].wait_recv()
-        a, b, d, ra, rb, last_square = (in_edge[0, g, i] for i in range(PARTS))
+        near_edges[g].wait_recv()
+        a, b, d, ra, rb, last_square = (near_in[g, i] for i in range(PARTS))
 
         def forward(k, carry, es=es):
             front, partial, last_square = carry
@@ -178,47 +185,49 @@
 
     alone = (me == 0) | (me == count - 1)
     sky_copies = []
-    for g in range(EXPO // GROUP):
-        es = pl.ds(g * GROUP, GROUP)
-        edges[1, g].wait_recv()
-        a2, b2, d2, ra2, rb2, next_square = (jnp.where(alone, 0.0, in_edge[1, g, i]) for i in range(PARTS))
+    for q in range(LATE):
+        es = pl.ds(q * SLICE, SLICE)
+        g, low = divmod(q * SLICE, GROUP)
+        far_edges[q].wait_recv()
+        a2, b2, d2, ra2, rb2, next_square = (jnp.where(alone, 0.0, far_in[q, i]) for i in range(PARTS))
         (a, b, d, ra, rb), partial = fronts[g]
+        a, b, d, ra, rb, partial = (v[low : low + SLICE] for v in (a, b, d, ra, rb, partial))
         prec[es, ROWS] = partial + next_square
         b = b + b2
         inverse = 1.0 / (a + d2 + REG)
         factor, base = b * inverse, (ra + rb2) * inverse
         beyond = (rb + ra2 - b * base) / (d + a2 + REG - factor * b)
         edge_flux = base - factor * beyond
-        flux[es, first_row + row_step * (ROWS - 1)] = edge_flux
-
-        def backward(i, carry, es=es):
-            next_one, next_two = carry
+
+        def sky_row(k, value, top, bottom, es=es):
+            n = first_row + row_step * k
+            flux[es, n] = value
+            share = prec[es, k + 1] * is_sky
+            return jnp.where(lane4 == n, fold(share * value), top), jnp.where(lane4 == n, fold(share), bottom)
+
+        def backward(i, carry, es=es, sky_row=sky_row):
+            next_one, next_two, top, bottom = carry
             k = ROWS - 1 - i
             value = start[es, k] - near[es, k] * next_one - far[es, k] * next_two
-            flux[es, first_row + row_step * (k - 1)] = value
-            return value, next_one
-
-        lax.fori_loop(0, ROWS - 1, backward, (edge_flux, beyond), unroll=7)
-
-        def sky_row(k, carry, es=es):
-            top, bottom = carry
-            n = first_row + row_step * k
-            share = prec[es, k + 1] * is_sky
-            scaled = share * flux[es, n]
-            return jnp.where(lane8 == n, fold(scaled), top), jnp.where(lane8 == n, fold(share), bottom)
-
-        sums[g, 0], sums[g, 1] = lax.fori_loop(0, ROWS, sky_row, (zero8, zero8), unroll=10)
-        sky_copies.append(
-            [
-                send(
-                    sums.at[g], boxes.at[g, specs - 1 - d], spec_send.at[g, d - 1], spec_recv.at[g, specs - 1 - d],
-                    {"spec": lax.rem(spec + d, specs)},
-                )
-                for d in range(1, specs)
-            ]
-        )
-        for copy in sky_copies[g]:
-            copy.start()
+            top, bottom = sky_row(k, next_one, top, bottom)
+            return value, next_one, top, bottom
+
+        value, _, top, bottom = lax.fori_loop(0, ROWS - 1, backward, (edge_flux, beyond, zero4, zero4), unroll=7)
+        top, bottom = sky_row(0, value, top, bottom)
+        sums[g, 0, low * PAIR : (low + SLICE) * PAIR] = top
+        sums[g, 1, low * PAIR : (low + SLICE) * PAIR] = bottom
+        if low + SLICE == GROUP:
+            sky_copies.append(
+                [
+                    send(
+                        sums.at[g], boxes.at[g, specs - 1 - d], spec_send.at[g, d - 1], spec_recv.at[g, specs - 1 - d],
+                        {"spec": lax.rem(spec + d, specs)},
+                    )
+                    for d in range(1, specs)
+                ]
+            )
+            for copy in sky_copies[g]:
+                copy.start()
 
     scale = 2.0 / (count * ROWS - 1)
     base_row = me * ROWS
@@ -262,61 +271,71 @@
         )
         for i in range(GROUP):
             e = g * GROUP + i
-            load[e, :, 0:F] = first[i]
-            load[e, :, WIDE : WIDE + F] = second[i]
-            load[e, :, 2 * WIDE : LOAD] = moment[i]
+            for half, width in ((0, HALF), (1, F - HALF)):
+                load[e, half, :, 0:width] = first[i][:, half * HALF : half * HALF + width]
+                load[e, half, :, HALF : HALF + width] = second[i][:, half * HALF : half * HALF + width]
+                load[e, half, :, WIDE:LOAD] = moment[i]
+        for t in range(PLANE):
+            where = ((t // CORES) * LINE + col) * CORES + t % CORES
+            slot = lax.rem(mem - t + PLANE, PLANE) - 1
+
+            @pl.when(mem != t)
+            def _(t=t, where=where, slot=slot, g=g):
+                source = load.at[g * GROUP + t % GROUP, t // GROUP]
+                send(source, box_a.at[g, slot], a_send.at[g], a_recv.at[g], {"wave": where}).start()
+
+    groups = range(EXPO // GROUP)
+    whole_a = [send(box_a.at[g], box_a.at[g], a_send.at[g], a_recv.at[g], {"wave": partner}) for g in groups]
+    whole_b = [send(box_b.at[g], box_b.at[g], b_send.at[g], b_recv.at[g], {"wave": partner}) for g in groups]
+    whole_c = []
+    for g in groups:
+        seven = gathered.at[g, pl.ds(0, PLANE - 1)]
+        whole_c.append(send(seven, seven, c_send.at[g], c_recv.at[g], {"wave": partner}))
+    for g in groups:
+        whole_a[g].wait_recv()
+        acc = load[g * GROUP + lax.rem(mem, GROUP), lax.div(mem, GROUP)]
+        for k in range(PLANE - 1):
+            acc = acc + box_a[g, k]
+        part[g] = acc
+        for d in FAR_FIRST:
+            send(part.at[g], box_b.at[g, LINE - 1 - d], b_send.at[g], b_recv.at[g], {"wave": line_peer(d)}).start()
+    for g in groups:
+        whole_b[g].wait_recv()
+        acc = part[g]
+        for k in range(LINE - 1):
+            acc = acc + box_b[g, k]
+        first_sum, second_sum, powers_sum = acc[:, :HALF], acc[:, HALF:WIDE], acc[:, WIDE:LOAD]
+
+        def pick(i, powers_sum=powers_sum):
+            return jnp.sum(jnp.where(lane2 == i, powers_sum, 0.0), axis=1, keepdims=True)
+
+        upper, cross, lower = pick(0) + RIDGE, pick(1), pick(2) + RIDGE
+        inverse = 1.0 / (upper * lower - cross * cross)
+        piece[g, 0] = (lower * first_sum - cross * second_sum) * inverse
+        piece[g, 1] = (upper * second_sum - cross * first_sum) * inverse
+        for d in FAR_FIRST:
+            send(piece.at[g], gathered.at[g, mem], c_send.at[g], c_recv.at[g], {"wave": plane_peer(d)[1]}).start()
+        gathered[g, mem] = piece[g]
+    for g in groups:
+        whole_c[g].wait_recv()
+        slope_a, slope_b = [], []
         for i in range(GROUP):
-            e = g * GROUP + i
-            where = ((e // CORES) * LINE + col) * CORES + e % CORES
-            slot = lax.rem(mem - e + PLANE, PLANE) - 1
-
-            @pl.when(mem != e)
-            def _(e=e, where=where, slot=slot):
-                send(load.at[e], box_a.at[slot], a_send, a_recv, {"wave": where}).start()
-
-    whole_a = send(box_a, box_a, a_send, a_recv, {"wave": partner})
-    whole_a.wait_recv()
-    acc = load[mem]
-    for k in range(PLANE - 1):
-        acc = acc + box_a[k]
-    part[...] = acc
-    for d in FAR_FIRST:
-        send(part, box_b.at[LINE - 1 - d], b_send, b_recv, {"wave": line_peer(d)}).start()
-    whole_b = send(box_b, box_b, b_send, b_recv, {"wave": partner})
-    whole_b.wait_recv()
-    for k in range(LINE - 1):
-        acc = acc + box_b[k]
-    first_sum, second_sum, powers_sum = acc[:, :WIDE], acc[:, WIDE : 2 * WIDE], acc[:, 2 * WIDE : LOAD]
-
-    def pick(i):
-        return jnp.sum(jnp.where(lane2 == i, powers_sum, 0.0), axis=1, keepdims=True)
-
-    upper, cross, lower = pick(0) + RIDGE, pick(1), pick(2) + RIDGE
-    inverse = 1.0 / (upper * lower - cross * cross)
-    piece[0] = (lower * first_sum - cross * second_sum) * inverse
-    piece[1] = (upper * second_sum - cross * first_sum) * inverse
-    slope_ref[mem] = piece[...]
-    for d in FAR_FIRST:
-        send(piece, slope_ref.at[mem], c_send, c_recv, {"wave": plane_peer(d)[1]}).start()
-    whole_c = send(slope_ref.at[pl.ds(0, PLANE - 1)], slope_ref.at[pl.ds(0, PLANE - 1)], c_send, c_recv, {"wave": partner})
-    whole_c.wait_recv()
-
-    slope_a = [slope_ref[e, 0, :, 0:F] for e in range(EXPO)]
-    slope_b = [slope_ref[e, 1, :, 0:F] for e in range(EXPO)]
-
-    def clean(n, carry):
-        place = (base_row + n).astype(f32) * scale - 1.0
-        for e in range(EXPO):
-            fitted = slope_a[e] + slope_b[e] * place
-            flux[e, n] = flux[e, n] - fitted * model_s[e // GROUP, e % GROUP, n]
-        return carry
-
-    lax.fori_loop(0, ROWS, clean, 0, unroll=5)
-    for copy in list(edges.values()) + sky_copies[0] + sky_copies[1]:
+            for half in range(2):
+                slope_ref[i, :, :, half * HALF : (half + 1) * HALF] = gathered[g, half * GROUP + i]
+            slope_a.append(slope_ref[i, 0, :, 0:F])
+            slope_b.append(slope_ref[i, 1, :, 0:F])
+
+        def clean(n, carry, g=g, slope_a=slope_a, slope_b=slope_b):
+            place = (base_row + n).astype(f32) * scale - 1.0
+            for i in range(GROUP):
+                fitted = slope_a[i] + slope_b[i] * place
+                e = g * GROUP + i
+                flux[e, n] = flux[e, n] - fitted * model_s[g, i, n]
+            return carry
+
+        lax.fori_loop(0, ROWS, clean, 0, unroll=5)
+    for copy in far_edges + near_edges + sky_copies[0] + sky_copies[1] + whole_a + whole_b + whole_c:
         copy.wait_send()
-    whole_a.wait_send()
-    whole_b.wait_send()
-    whole_c.wait_send()
 
 
 def store_kernel(cleaned, model, cleaned_out, model_out, model_rows, sems):
@@ -337,7 +356,7 @@
     hbm, vmem = pl.BlockSpec(memory_space=pltpu.HBM), pl.BlockSpec(memory_space=pltpu.VMEM)
     dma = pltpu.SemaphoreType.DMA
     groups = EXPO // GROUP
-    edge = (2, groups, PARTS, GROUP, PAIR, F)
+    near_edge, far_edge = (groups, PARTS, GROUP, PAIR, F), (LATE, PARTS, SLICE, PAIR, F)
     cleaned, model = pl.pallas_call(
         main_kernel,
         out_shape=(
@@ -355,30 +374,35 @@
             pltpu.VMEM(field, f32),
             pltpu.VMEM(field, f32),
             pltpu.VMEM((EXPO, ROWS + 1, PAIR, F), f32),
-            pltpu.VMEM(edge, f32),
-            pltpu.VMEM(edge, f32),
+            pltpu.VMEM(near_edge, f32),
+            pltpu.VMEM(near_edge, f32),
+            pltpu.VMEM(far_edge, f32),
+            pltpu.VMEM(far_edge, f32),
             pltpu.VMEM((groups, 2, GROUP * PAIR, 128), f32),
             pltpu.VMEM((groups, specs - 1, 2, GROUP * PAIR, 128), f32),
             pltpu.VMEM((groups, GROUP, 128), f32),
             pltpu.SMEM((groups, GROUP, 128), f32),
-            pltpu.VMEM((EXPO, PAIR, LOAD), f32),
-            pltpu.VMEM((PLANE - 1, PAIR, LOAD), f32),
-            pltpu.VMEM((PAIR, LOAD), f32),
-            pltpu.VMEM((LINE - 1, PAIR, LOAD), f32),
-            pltpu.VMEM((2, PAIR, WIDE), f32),
-            pltpu.VMEM((EXPO, 2, PAIR, WIDE), f32),
+            pltpu.VMEM((EXPO, 2, PAIR, LOAD), f32),
+            pltpu.VMEM((groups, PLANE - 1, PAIR, LOAD), f32),
+            pltpu.VMEM((groups, PAIR, LOAD), f32),
+            pltpu.VMEM((groups, LINE - 1, PAIR, LOAD), f32),
+            pltpu.VMEM((groups, 2, PAIR, HALF), f32),
+            pltpu.VMEM((groups, PLANE, 2, PAIR, HALF), f32),
+            pltpu.VMEM((GROUP, 2, PAIR, WIDE), f32),
             dma((3, 5)),
-            dma((2, groups)),
-            dma((2, groups)),
+            dma((groups,)),
+            dma((groups,)),
+            dma((LATE,)),
+            dma((LATE,)),
             dma((groups, specs - 1)),
             dma((groups, specs - 1)),
             dma,
-            dma,
-            dma,
-            dma,
-            dma,
-            dma,
-            dma,
+            dma((groups,)),
+            dma((groups,)),
+            dma((groups,)),
+            dma((groups,)),
+            dma((groups,)),
+            dma((groups,)),
         ],
         compiler_params=pltpu.CompilerParams(
             collective_id=0, has_side_effects=True, vmem_limit_bytes=54_000_000

time: 36.2 us -> 37.6 us (1.039)
  Pallas kernels: 35.5 us -> 36.9 us
    pallas_call x1, Pallas kernels: 34.2 us -> 35.6 us  [local(): pl.pallas_call(main_kernel, out_shape=(jax.ShapeDtypeStruct(field, f32),...]
where the time goes in v6:
time: 37.6 us; the launch traced here: 37.5 us
  Pallas kernels  36.9 us (98%)
  between operations  0.64 us (2%)
    pallas_call x1, Pallas kernels, local(): pl.pallas_call(main_kernel, out_shape=(jax.ShapeDtypeStruct(field, f32),...  35.6 us
    pallas_call x1, Pallas kernels, local(): pl.pallas_call(store_kernel, out_shape=(jax.ShapeDtypeStruct(field, f32),...  1.24 us

profile of v6, /device:TPU:1, one launch (start us, length us, event | category | flops | bytes accessed | tf_op | source)
XLA Modules:
  0.0 37.5 jit_solution(8923286863352696977)
XLA Ops:
  0.6 35.6 %deconvolve.1 = (f32[8,50,2,500]{3,2,1,0:T(2,128)S(1)}, f32[8,128]{1,0:T(8,128)S(1)}) custom-call(f32[8,50,2,500]{3,2,1,0:T(2,128)} %bitcast.6, f32[8,50,2,500]{3,2,1,0:T(2,128)} %bitcast.7, s32[8,50,2,500]{3,2,1,0:T(2,128)} %bitcast.8, f32[8,50,2,500]{3,2,1,0:T(2,128)} %bitcast.9, f32[8,50,2,500]{3,2,1,0:T(2,128)} %bitcast.10, s32[2,40]{1,0:T(2,128)} %index.1), custom_call_target="tpu_custom_call" | custom-call | tf_op jit(solution)/shard_map/deconvolve/pallas_call | solution.py:360
  36.3 1.2 %store.1 = (f32[8,50,2,500]{3,2,1,0:T(2,128)}, f32[8,50]{1,0:T(8,128)}) custom-call(f32[8,50,2,500]{3,2,1,0:T(2,128)S(1)} %get-tuple-element.6.cleaned, f32[8,128]{1,0:T(8,128)S(1)} %get-tuple-element.7.model), custom_call_target="tpu_custom_call" | custom-call | tf_op jit(solution)/shard_map/store/pallas_call | solution.py:412

commit v7 on v5

--- a/solution.py
+++ b/solution.py
@@ -54,7 +54,7 @@
     px, iv, mk, lr, near, far, start, prec,
     out_edge, in_edge, sums, boxes, model_v, model_s, load, box_a, part, box_b, piece, slope_ref,
     load_sem, edge_send, edge_recv, spec_send, spec_recv, smem_sem,
-    a_send, a_recv, b_send, b_recv, c_send, c_recv,
+    a_send, a_recv, b_send, b_recv, c_send, c_recv, known_one, known_two,
 ):
     me = lax.axis_index("wave")
     count = lax.axis_size("wave")
@@ -82,11 +82,14 @@
 
     hbm = (iv_hbm, mk_hbm, lf_hbm, rt_hbm, px_hbm)
     vmem = (iv, mk, lr.at[0], lr.at[1], px)
-    spans = (pl.ds(ROWS - EDGE, EDGE), pl.ds(0, EDGE), pl.ds(EDGE, ROWS - 2 * EDGE))
+    spans = (pl.ds((ROWS - EDGE) * core, EDGE), pl.ds((ROWS - EDGE) * (1 - core), EDGE), pl.ds(EDGE, ROWS - 2 * EDGE))
+    everything = pl.ds(0, EXPO)
+    cuts = [(everything, span) for span in spans[:2]] + [(pl.ds(g * GROUP, GROUP), spans[2]) for g in range(EXPO // GROUP)]
     loads = [
-        [pltpu.make_async_copy(h.at[:, span], v.at[:, span], load_sem.at[i, j]) for j, (h, v) in enumerate(zip(hbm, vmem))]
-        for i, span in enumerate(spans)
+        [pltpu.make_async_copy(h.at[cut], v.at[cut], load_sem.at[i, j]) for j, (h, v) in enumerate(zip(hbm, vmem))]
+        for i, cut in enumerate(cuts)
     ]
+
     barrier = pltpu.get_barrier_semaphore()
 
     def greet(peers):
@@ -94,13 +97,13 @@
             pl.semaphore_signal(barrier, inc=1, device_id=peer, device_id_type=MESH)
         return len(peers)
 
-    greeted = greet([{"wave": line_peer(d)} for d in FAR_FIRST])
-    for group in loads[:2]:
+    greeted = greet([{"wave": outside}, {"wave": partner}])
+    for group in loads[:3]:
         for copy in group:
             copy.start()
     greeted += greet([{"wave": plane_peer(d)[1]} for d in FAR_FIRST])
-    greeted += greet([{"spec": lax.rem(spec + d, specs)} for d in range(1, specs)])
-    greeted += greet([{"wave": outside}, {"wave": partner}])
+    greeted += greet([{"spec": lax.rem(spec + d, specs)} for d in (2, 1, 3)])
+    greeted += greet([{"wave": line_peer(1)}, {"wave": line_peer(LINE - 1)}])
 
     def weight_of(es, n):
         return iv[es, n] * (1.0 - mk[es, n].astype(f32))
@@ -119,33 +122,38 @@
         for i, value in enumerate(front + (inner_square,)):
             out_edge[side, g, i] = value
 
-    for group in loads[:2]:
-        for copy in group:
-            copy.wait()
-    for copy in loads[2]:
+    edges = {}
+
+    def hand_over(side, g):
+        copy = send(
+            out_edge.at[side, g], in_edge.at[side, g], edge_send.at[side, g], edge_recv.at[side, g],
+            {"wave": sides[side][3]},
+        )
         copy.start()
+        edges[side, g] = copy
+
+    for copy in loads[3]:
+        copy.start()
+    for copy in loads[0]:
+        copy.wait()
     for g in range(EXPO // GROUP):
-        for side in (1, 0):
-            reduce_edge(side, g)
-
-    pl.semaphore_wait(barrier, greeted)
-    edges = {}
+        reduce_edge(1, g)
+        if g == 0:
+            pl.semaphore_wait(barrier, greeted)
+        hand_over(1, g)
+    for copy in loads[1]:
+        copy.wait()
     for g in range(EXPO // GROUP):
-        for side in (1, 0):
-            copy = send(
-                out_edge.at[side, g], in_edge.at[side, g], edge_send.at[side, g], edge_recv.at[side, g],
-                {"wave": sides[side][3]},
-            )
-            copy.start()
-            edges[side, g] = copy
+        reduce_edge(0, g)
+        hand_over(0, g)
+    for d in (1, LINE - 1):
+        pl.semaphore_signal(known_one, inc=1, device_id={"wave": line_peer(d)}, device_id_type=MESH)
     fibre = lax.broadcasted_iota(jnp.int32, (PAIR, F), 1)
     second_row = lax.broadcasted_iota(jnp.int32, (PAIR, F), 0) == 1
     is_sky = jnp.zeros((PAIR, F), f32)
     for j in range(index.shape[1]):
         is_sky = is_sky + jnp.where(fibre == jnp.where(second_row, index[1, j], index[0, j]), 1.0, 0.0)
     is_sky = is_sky[None]
-    for copy in loads[2]:
-        copy.wait()
 
     lane8 = lax.broadcasted_iota(jnp.int32, (GROUP * PAIR, 128), 1)
     zero8 = jnp.zeros((GROUP * PAIR, 128), f32)
@@ -157,6 +165,8 @@
     fronts = []
     for g in range(EXPO // GROUP):
         es = pl.ds(g * GROUP, GROUP)
+        for copy in loads[2 + g]:
+            copy.wait()
         edges[0, g].wait_recv()
         a, b, d, ra, rb, last_square = (in_edge[0, g, i] for i in range(PARTS))
 
@@ -176,6 +186,9 @@
         )
         fronts.append((front, partial))
 
+    pl.semaphore_wait(known_one, 2)
+    for d in (2, LINE - 2):
+        pl.semaphore_signal(known_two, inc=1, device_id={"wave": line_peer(d)}, device_id_type=MESH)
     alone = (me == 0) | (me == count - 1)
     sky_copies = []
     for g in range(EXPO // GROUP):
@@ -207,7 +220,7 @@
             scaled = share * flux[es, n]
             return jnp.where(lane8 == n, fold(scaled), top), jnp.where(lane8 == n, fold(share), bottom)
 
-        sums[g, 0], sums[g, 1] = lax.fori_loop(0, ROWS, sky_row, (zero8, zero8), unroll=10)
+        sums[g, 0], sums[g, 1] = lax.fori_loop(0, ROWS, sky_row, (zero8, zero8), unroll=25)
         sky_copies.append(
             [
                 send(
@@ -276,6 +289,7 @@
 
     whole_a = send(box_a, box_a, a_send, a_recv, {"wave": partner})
     whole_a.wait_recv()
+    pl.semaphore_wait(known_two, 2)
     acc = load[mem]
     for k in range(PLANE - 1):
         acc = acc + box_a[k]
@@ -367,7 +381,7 @@
             pltpu.VMEM((LINE - 1, PAIR, LOAD), f32),
             pltpu.VMEM((2, PAIR, WIDE), f32),
             pltpu.VMEM((EXPO, 2, PAIR, WIDE), f32),
-            dma((3, 5)),
+            dma((2 + groups, 5)),
             dma((2, groups)),
             dma((2, groups)),
             dma((groups, specs - 1)),
@@ -379,6 +393,8 @@
             dma,
             dma,
             dma,
+            pltpu.SemaphoreType.REGULAR,
+            pltpu.SemaphoreType.REGULAR,
         ],
         compiler_params=pltpu.CompilerParams(
             collective_id=0, has_side_effects=True, vmem_limit_bytes=54_000_000

time: 36.2 us -> 34.8 us (0.961)
  Pallas kernels: 35.5 us -> 34.1 us
    pallas_call x1, Pallas kernels: 34.2 us -> 32.9 us  [local(): pl.pallas_call(main_kernel, out_shape=(jax.ShapeDtypeStruct(field, f32),...]
where the time goes in v7:
time: 34.8 us
  Pallas kernels  34.1 us (98%)
  between operations  0.64 us (2%)
    pallas_call x1, Pallas kernels, local(): pl.pallas_call(main_kernel, out_shape=(jax.ShapeDtypeStruct(field, f32),...  32.9 us
    pallas_call x1, Pallas kernels, local(): pl.pallas_call(store_kernel, out_shape=(jax.ShapeDtypeStruct(field, f32),...  1.24 us

profile of v7, /device:TPU:1, one launch (start us, length us, event | category | flops | bytes accessed | tf_op | source)
XLA Modules:
  0.0 34.8 jit_solution(2434407781329604652)
XLA Ops:
  0.6 32.9 %deconvolve.1 = (f32[8,50,2,500]{3,2,1,0:T(2,128)S(1)}, f32[8,128]{1,0:T(8,128)S(1)}) custom-call(f32[8,50,2,500]{3,2,1,0:T(2,128)} %bitcast.6, f32[8,50,2,500]{3,2,1,0:T(2,128)} %bitcast.7, s32[8,50,2,500]{3,2,1,0:T(2,128)} %bitcast.8, f32[8,50,2,500]{3,2,1,0:T(2,128)} %bitcast.9, f32[8,50,2,500]{3,2,1,0:T(2,128)} %bitcast.10, s32[2,40]{1,0:T(2,128)} %index.1), custom_call_target="tpu_custom_call" | custom-call | tf_op jit(solution)/shard_map/deconvolve/pallas_call | solution.py:355
  33.5 1.2 %store.1 = (f32[8,50,2,500]{3,2,1,0:T(2,128)}, f32[8,50]{1,0:T(8,128)}) custom-call(f32[8,50,2,500]{3,2,1,0:T(2,128)S(1)} %get-tuple-element.6.cleaned, f32[8,128]{1,0:T(8,128)S(1)} %get-tuple-element.7.model), custom_call_target="tpu_custom_call" | custom-call | tf_op jit(solution)/shard_map/store/pallas_call | solution.py:404

commit v8 on v7

--- a/solution.py
+++ b/solution.py
@@ -30,10 +30,11 @@
     a, b, d, ra, rb = front
     w_outer, w_inner, w_pixel = weight * outer, weight * inner, weight * pixel
     outer_square, inner_square = w_outer * outer, w_inner * inner
-    a = a + outer_square + REG
+    own = weight + REG
+    a = a + outer_square
     b = b + w_outer
     far = w_outer * inner
-    d = d + weight
+    d = d + own
     ra = ra + outer * w_pixel
     rb = rb + w_pixel
     inverse = 1.0 / a
@@ -45,15 +46,15 @@
         rb - b * start,
         inner * w_pixel - far * start,
     )
-    return front, (near_factor, far_factor, start), outer_square, inner_square
+    return front, (near_factor, far_factor, start), outer_square, inner_square, own
 
 
 def main_kernel(
-    px_hbm, iv_hbm, mk_hbm, lf_hbm, rt_hbm, index,
+    px_hbm, iv_hbm, mk_hbm, lf_hbm, rt_hbm, index_hbm,
     flux, model_ref,
-    px, iv, mk, lr, near, far, start, prec,
+    px, iv, mk, lr, index, near, far, start, prec,
     out_edge, in_edge, sums, boxes, model_v, model_s, load, box_a, part, box_b, piece, slope_ref,
-    load_sem, edge_send, edge_recv, spec_send, spec_recv, smem_sem,
+    load_sem, index_sem, edge_send, edge_recv, spec_send, spec_recv, smem_sem,
     a_send, a_recv, b_send, b_recv, c_send, c_recv, known_one, known_two,
 ):
     me = lax.axis_index("wave")
@@ -106,7 +107,7 @@
     greeted += greet([{"wave": line_peer(1)}, {"wave": line_peer(LINE - 1)}])
 
     def weight_of(es, n):
-        return iv[es, n] * (1.0 - mk[es, n].astype(f32))
+        return jnp.where(mk[es, n] == 0, iv[es, n], 0.0)
 
     sides = ((46 - 43 * core, 1 - 2 * core, core, partner), (3 + 43 * core, 2 * core - 1, 1 - core, outside))
 
@@ -115,10 +116,10 @@
         es = pl.ds(g * GROUP, GROUP)
         weight, inner = weight_of(es, base), lr[1 - outer, es, base]
         w_inner, w_pixel = weight * inner, weight * px[es, base]
-        front = (weight, w_inner, w_inner * inner, w_pixel, inner * w_pixel)
+        front = (weight + REG, w_inner, w_inner * inner, w_pixel, inner * w_pixel)
         for i in range(1, EDGE):
             n = base + step * i
-            front, _, _, inner_square = absorb(front, weight_of(es, n), lr[outer, es, n], lr[1 - outer, es, n], px[es, n])
+            front, _, _, inner_square, _ = absorb(front, weight_of(es, n), lr[outer, es, n], lr[1 - outer, es, n], px[es, n])
         for i, value in enumerate(front + (inner_square,)):
             out_edge[side, g, i] = value
 
@@ -134,6 +135,8 @@
 
     for copy in loads[3]:
         copy.start()
+    index_copy = pltpu.make_async_copy(index_hbm, index, index_sem)
+    index_copy.start()
     for copy in loads[0]:
         copy.wait()
     for g in range(EXPO // GROUP):
@@ -149,6 +152,7 @@
     for d in (1, LINE - 1):
         pl.semaphore_signal(known_one, inc=1, device_id={"wave": line_peer(d)}, device_id_type=MESH)
     fibre = lax.broadcasted_iota(jnp.int32, (PAIR, F), 1)
+    index_copy.wait()
     second_row = lax.broadcasted_iota(jnp.int32, (PAIR, F), 0) == 1
     is_sky = jnp.zeros((PAIR, F), f32)
     for j in range(index.shape[1]):
@@ -174,12 +178,12 @@
             front, partial, last_square = carry
             n = first_row + row_step * k
             weight = weight_of(es, n)
-            front, factors, outer_square, inner_square = absorb(
+            front, factors, outer_square, inner_square, own = absorb(
                 front, weight, lr[1 - core, es, n], lr[core, es, n], px[es, n]
             )
             prec[es, k] = partial + outer_square
             near[es, k], far[es, k], start[es, k] = factors
-            return front, weight + last_square + REG, inner_square
+            return front, own + last_square, inner_square
 
         front, partial, _ = lax.fori_loop(
             0, ROWS, forward, ((a, b, d, ra, rb), jnp.zeros_like(a), last_square), unroll=5
@@ -194,13 +198,15 @@
     for g in range(EXPO // GROUP):
         es = pl.ds(g * GROUP, GROUP)
         edges[1, g].wait_recv()
-        a2, b2, d2, ra2, rb2, next_square = (jnp.where(alone, 0.0, in_edge[1, g, i]) for i in range(PARTS))
+        a2, b2, d2, ra2, rb2, next_square = (
+            jnp.where(alone, 0.0 if i else REG, in_edge[1, g, i]) for i in range(PARTS)
+        )
         (a, b, d, ra, rb), partial = fronts[g]
         prec[es, ROWS] = partial + next_square
         b = b + b2
-        inverse = 1.0 / (a + d2 + REG)
+        inverse = 1.0 / (a + d2)
         factor, base = b * inverse, (ra + rb2) * inverse
-        beyond = (rb + ra2 - b * base) / (d + a2 + REG - factor * b)
+        beyond = (rb + ra2 - b * base) / (d + a2 - factor * b)
         edge_flux = base - factor * beyond
         flux[es, first_row + row_step * (ROWS - 1)] = edge_flux
 
@@ -334,14 +340,13 @@
 
 
 def store_kernel(cleaned, model, cleaned_out, model_out, model_rows, sems):
-    copies = [pltpu.make_async_copy(cleaned.at[e], cleaned_out.at[e], sems.at[e]) for e in range(EXPO)]
-    for copy in copies:
-        copy.start()
+    main = pltpu.make_async_copy(cleaned, cleaned_out, sems.at[0])
+    main.start()
     model_rows[...] = model[:, 0:ROWS]
-    copies.append(pltpu.make_async_copy(model_rows, model_out, sems.at[EXPO]))
-    copies[-1].start()
-    for copy in copies:
-        copy.wait()
+    small = pltpu.make_async_copy(model_rows, model_out, sems.at[1])
+    small.start()
+    small.wait()
+    main.wait()
 
 
 def local(pixels, ivar, mask, psf_left, psf_right, sky_index):
@@ -358,13 +363,14 @@
             jax.ShapeDtypeStruct(field, f32),
             jax.ShapeDtypeStruct((EXPO, 128), f32),
         ),
-        in_specs=[hbm] * 5 + [pl.BlockSpec(memory_space=pltpu.SMEM)],
+        in_specs=[hbm] * 6,
         out_specs=(vmem, vmem),
         scratch_shapes=[
             pltpu.VMEM(field, f32),
             pltpu.VMEM(field, f32),
             pltpu.VMEM(field, jnp.int32),
             pltpu.VMEM((2,) + field, f32),
+            pltpu.SMEM(sky_index.shape, jnp.int32),
             pltpu.VMEM(field, f32),
             pltpu.VMEM(field, f32),
             pltpu.VMEM(field, f32),
@@ -382,6 +388,7 @@
             pltpu.VMEM((2, PAIR, WIDE), f32),
             pltpu.VMEM((EXPO, 2, PAIR, WIDE), f32),
             dma((2 + groups, 5)),
+            dma,
             dma((2, groups)),
             dma((2, groups)),
             dma((groups, specs - 1)),
@@ -406,7 +413,7 @@
         out_shape=(jax.ShapeDtypeStruct(field, f32), jax.ShapeDtypeStruct((EXPO, ROWS), f32)),
         in_specs=[vmem, vmem],
         out_specs=(hbm, hbm),
-        scratch_shapes=[pltpu.VMEM((EXPO, ROWS), f32), dma((EXPO + 1,))],
+        scratch_shapes=[pltpu.VMEM((EXPO, ROWS), f32), dma((2,))],
         compiler_params=pltpu.CompilerParams(vmem_limit_bytes=54_000_000),
         name="store",
     )(cleaned, model)

time: 34.8 us -> 34.1 us (0.980)
  Pallas kernels: 34.1 us -> 33.4 us
    pallas_call x1, Pallas kernels: 32.9 us -> 32.2 us  [local(): pl.pallas_call(main_kernel, out_shape=(jax.ShapeDtypeStruct(field, f32),...]
where the time goes in v8:
time: 34.1 us; the launch traced here: 34 us
  Pallas kernels  33.4 us (98%)
  between operations  0.64 us (2%)
    pallas_call x1, Pallas kernels, local(): pl.pallas_call(main_kernel, out_shape=(jax.ShapeDtypeStruct(field, f32),...  32.2 us
    pallas_call x1, Pallas kernels, local(): pl.pallas_call(store_kernel, out_shape=(jax.ShapeDtypeStruct(field, f32),...  1.18 us

profile of v8, /device:TPU:1, one launch (start us, length us, event | category | flops | bytes accessed | tf_op | source)
XLA Modules:
  0.0 34.0 jit_solution(6310422175905357182)
XLA Ops:
  0.6 32.2 %deconvolve.1 = (f32[8,50,2,500]{3,2,1,0:T(2,128)S(1)}, f32[8,128]{1,0:T(8,128)S(1)}) custom-call(f32[8,50,2,500]{3,2,1,0:T(2,128)} %bitcast.6, f32[8,50,2,500]{3,2,1,0:T(2,128)} %bitcast.7, s32[8,50,2,500]{3,2,1,0:T(2,128)} %bitcast.8, f32[8,50,2,500]{3,2,1,0:T(2,128)} %bitcast.9, f32[8,50,2,500]{3,2,1,0:T(2,128)} %bitcast.10, s32[2,40]{1,0:T(2,128)} %index_hbm.1), custom_call_target="tpu_custom_call" | custom-call | tf_op jit(solution)/shard_map/deconvolve/pallas_call | solution.py:360
  32.8 1.2 %store.1 = (f32[8,50,2,500]{3,2,1,0:T(2,128)}, f32[8,50]{1,0:T(8,128)}) custom-call(f32[8,50,2,500]{3,2,1,0:T(2,128)S(1)} %get-tuple-element.6.cleaned, f32[8,128]{1,0:T(8,128)S(1)} %get-tuple-element.7.model), custom_call_target="tpu_custom_call" | custom-call | tf_op jit(solution)/shard_map/store/pallas_call | solution.py:411

commit v9 on v8

--- a/solution.py
+++ b/solution.py
@@ -20,7 +20,9 @@
 PLANE = 8
 GROUP = 4
 PARTS = 6
-LOAD = 2 * WIDE + 128
+LOAD = 2 * WIDE
+TILE = WIDE - 128
+SPARE = F - TILE
 FAR_FIRST = (4, 3, 5, 2, 6, 1, 7)
 
 f32 = jnp.float32
@@ -133,22 +135,20 @@
         copy.start()
         edges[side, g] = copy
 
+    for copy in loads[0]:
+        copy.wait()
+    reduce_edge(1, 0)
+    pl.semaphore_wait(barrier, greeted)
+    hand_over(1, 0)
+    for copy in loads[1]:
+        copy.wait()
+    for side, g in ((0, 0), (1, 1), (0, 1)):
+        reduce_edge(side, g)
+        hand_over(side, g)
     for copy in loads[3]:
         copy.start()
     index_copy = pltpu.make_async_copy(index_hbm, index, index_sem)
     index_copy.start()
-    for copy in loads[0]:
-        copy.wait()
-    for g in range(EXPO // GROUP):
-        reduce_edge(1, g)
-        if g == 0:
-            pl.semaphore_wait(barrier, greeted)
-        hand_over(1, g)
-    for copy in loads[1]:
-        copy.wait()
-    for g in range(EXPO // GROUP):
-        reduce_edge(0, g)
-        hand_over(0, g)
     for d in (1, LINE - 1):
         pl.semaphore_signal(known_one, inc=1, device_id={"wave": line_peer(d)}, device_id_type=MESH)
     fibre = lax.broadcasted_iota(jnp.int32, (PAIR, F), 1)
@@ -267,7 +267,7 @@
         def regress(n, carry, g=g):
             first, second, moment = (list(v) for v in carry)
             place = (base_row + n).astype(f32) * scale - 1.0
-            powers = jnp.where(lane2 == 0, 1.0, jnp.where(lane2 == 1, place, place * place))
+            powers = jnp.where(lane2 == SPARE, 1.0, jnp.where(lane2 == SPARE + 1, place, place * place))
             for i in range(GROUP):
                 sky = model_s[g, i, n]
                 term = flux[g * GROUP + i, n] * sky
@@ -283,7 +283,7 @@
             e = g * GROUP + i
             load[e, :, 0:F] = first[i]
             load[e, :, WIDE : WIDE + F] = second[i]
-            load[e, :, 2 * WIDE : LOAD] = moment[i]
+            load[e, :, TILE:WIDE] = jnp.where(lane2 < SPARE, load[e, :, TILE:WIDE], moment[i])
         for i in range(GROUP):
             e = g * GROUP + i
             where = ((e // CORES) * LINE + col) * CORES + e % CORES
@@ -306,10 +306,10 @@
     whole_b.wait_recv()
     for k in range(LINE - 1):
         acc = acc + box_b[k]
-    first_sum, second_sum, powers_sum = acc[:, :WIDE], acc[:, WIDE : 2 * WIDE], acc[:, 2 * WIDE : LOAD]
+    first_sum, second_sum, powers_sum = acc[:, :WIDE], acc[:, WIDE:LOAD], acc[:, TILE:WIDE]
 
     def pick(i):
-        return jnp.sum(jnp.where(lane2 == i, powers_sum, 0.0), axis=1, keepdims=True)
+        return jnp.sum(jnp.where(lane2 == SPARE + i, powers_sum, 0.0), axis=1, keepdims=True)
 
     upper, cross, lower = pick(0) + RIDGE, pick(1), pick(2) + RIDGE
     inverse = 1.0 / (upper * lower - cross * cross)

time: 34.1 us -> 34 us (level)
  no operation moved by 1% of the time
where the time goes in v9:
time: 34 us; the launch traced here: 33.9 us
  Pallas kernels  33.3 us (98%)
  between operations  0.64 us (2%)
    pallas_call x1, Pallas kernels, local(): pl.pallas_call(main_kernel, out_shape=(jax.ShapeDtypeStruct(field, f32),...  32.1 us
    pallas_call x1, Pallas kernels, local(): pl.pallas_call(store_kernel, out_shape=(jax.ShapeDtypeStruct(field, f32),...  1.18 us

profile of v9, /device:TPU:1, one launch (start us, length us, event | category | flops | bytes accessed | tf_op | source)
XLA Modules:
  0.0 33.9 jit_solution(6747243622709933269)
XLA Ops:
  0.6 32.1 %deconvolve.1 = (f32[8,50,2,500]{3,2,1,0:T(2,128)S(1)}, f32[8,128]{1,0:T(8,128)S(1)}) custom-call(f32[8,50,2,500]{3,2,1,0:T(2,128)} %bitcast.6, f32[8,50,2,500]{3,2,1,0:T(2,128)} %bitcast.7, s32[8,50,2,500]{3,2,1,0:T(2,128)} %bitcast.8, f32[8,50,2,500]{3,2,1,0:T(2,128)} %bitcast.9, f32[8,50,2,500]{3,2,1,0:T(2,128)} %bitcast.10, s32[2,40]{1,0:T(2,128)} %index_hbm.1), custom_call_target="tpu_custom_call" | custom-call | tf_op jit(solution)/shard_map/deconvolve/pallas_call | solution.py:360
  32.7 1.2 %store.1 = (f32[8,50,2,500]{3,2,1,0:T(2,128)}, f32[8,50]{1,0:T(8,128)}) custom-call(f32[8,50,2,500]{3,2,1,0:T(2,128)S(1)} %get-tuple-element.6.cleaned, f32[8,128]{1,0:T(8,128)S(1)} %get-tuple-element.7.model), custom_call_target="tpu_custom_call" | custom-call | tf_op jit(solution)/shard_map/store/pallas_call | solution.py:411

commit v10 on v9

--- a/solution.py
+++ b/solution.py
@@ -100,8 +100,10 @@
             pl.semaphore_signal(barrier, inc=1, device_id=peer, device_id_type=MESH)
         return len(peers)
 
+    for copy in loads[0]:
+        copy.start()
     greeted = greet([{"wave": outside}, {"wave": partner}])
-    for group in loads[:3]:
+    for group in loads[1:3]:
         for copy in group:
             copy.start()
     greeted += greet([{"wave": plane_peer(d)[1]} for d in FAR_FIRST])
@@ -226,14 +228,14 @@
             scaled = share * flux[es, n]
             return jnp.where(lane8 == n, fold(scaled), top), jnp.where(lane8 == n, fold(share), bottom)
 
-        sums[g, 0], sums[g, 1] = lax.fori_loop(0, ROWS, sky_row, (zero8, zero8), unroll=25)
+        sums[g, 0], sums[g, 1] = lax.fori_loop(0, ROWS, sky_row, (zero8, zero8), unroll=50)
         sky_copies.append(
             [
                 send(
                     sums.at[g], boxes.at[g, specs - 1 - d], spec_send.at[g, d - 1], spec_recv.at[g, specs - 1 - d],
                     {"spec": lax.rem(spec + d, specs)},
                 )
-                for d in range(1, specs)
+                for d in (2, 1, 3)
             ]
         )
         for copy in sky_copies[g]:
@@ -284,14 +286,12 @@
             load[e, :, 0:F] = first[i]
             load[e, :, WIDE : WIDE + F] = second[i]
             load[e, :, TILE:WIDE] = jnp.where(lane2 < SPARE, load[e, :, TILE:WIDE], moment[i])
-        for i in range(GROUP):
-            e = g * GROUP + i
-            where = ((e // CORES) * LINE + col) * CORES + e % CORES
-            slot = lax.rem(mem - e + PLANE, PLANE) - 1
-
-            @pl.when(mem != e)
-            def _(e=e, where=where, slot=slot):
-                send(load.at[e], box_a.at[slot], a_send, a_recv, {"wave": where}).start()
+        for d in FAR_FIRST:
+            other, where = plane_peer(d)
+
+            @pl.when(lax.div(other, GROUP) == g)
+            def _(d=d, other=other, where=where):
+                send(load.at[other], box_a.at[PLANE - 1 - d], a_send, a_recv, {"wave": where}).start()
 
     whole_a = send(box_a, box_a, a_send, a_recv, {"wave": partner})
     whole_a.wait_recv()

time: 34 us -> 33.8 us (level)
  no operation moved by 1% of the time
where the time goes in v10:
time: 33.8 us; the launch traced here: 33.7 us
  Pallas kernels  33 us (98%)
  between operations  0.64 us (2%)
    pallas_call x1, Pallas kernels, local(): pl.pallas_call(main_kernel, out_shape=(jax.ShapeDtypeStruct(field, f32),...  31.8 us
    pallas_call x1, Pallas kernels, local(): pl.pallas_call(store_kernel, out_shape=(jax.ShapeDtypeStruct(field, f32),...  1.18 us

profile of v10, /device:TPU:1, one launch (start us, length us, event | category | flops | bytes accessed | tf_op | source)
XLA Modules:
  0.0 33.7 jit_solution(4259669824147885844)
XLA Ops:
  0.6 31.8 %deconvolve.1 = (f32[8,50,2,500]{3,2,1,0:T(2,128)S(1)}, f32[8,128]{1,0:T(8,128)S(1)}) custom-call(f32[8,50,2,500]{3,2,1,0:T(2,128)} %bitcast.6, f32[8,50,2,500]{3,2,1,0:T(2,128)} %bitcast.7, s32[8,50,2,500]{3,2,1,0:T(2,128)} %bitcast.8, f32[8,50,2,500]{3,2,1,0:T(2,128)} %bitcast.9, f32[8,50,2,500]{3,2,1,0:T(2,128)} %bitcast.10, s32[2,40]{1,0:T(2,128)} %index_hbm.1), custom_call_target="tpu_custom_call" | custom-call | tf_op jit(solution)/shard_map/deconvolve/pallas_call | solution.py:360
  32.5 1.2 %store.1 = (f32[8,50,2,500]{3,2,1,0:T(2,128)}, f32[8,50]{1,0:T(8,128)}) custom-call(f32[8,50,2,500]{3,2,1,0:T(2,128)S(1)} %get-tuple-element.6.cleaned, f32[8,128]{1,0:T(8,128)S(1)} %get-tuple-element.7.model), custom_call_target="tpu_custom_call" | custom-call | tf_op jit(solution)/shard_map/store/pallas_call | solution.py:411

commit v11 on v10

--- a/solution.py
+++ b/solution.py
@@ -219,7 +219,7 @@
             flux[es, first_row + row_step * (k - 1)] = value
             return value, next_one
 
-        lax.fori_loop(0, ROWS - 1, backward, (edge_flux, beyond), unroll=7)
+        lax.fori_loop(0, ROWS - 1, backward, (edge_flux, beyond), unroll=49)
 
         def sky_row(k, carry, es=es):
             top, bottom = carry
@@ -279,7 +279,7 @@
             return tuple(first), tuple(second), tuple(moment)
 
         first, second, moment = lax.fori_loop(
-            0, ROWS, regress, ((zero,) * GROUP, (zero,) * GROUP, (zero_moment,) * GROUP), unroll=5
+            0, ROWS, regress, ((zero,) * GROUP, (zero,) * GROUP, (zero_moment,) * GROUP), unroll=10
         )
         for i in range(GROUP):
             e = g * GROUP + i
@@ -331,7 +331,7 @@
             flux[e, n] = flux[e, n] - fitted * model_s[e // GROUP, e % GROUP, n]
         return carry
 
-    lax.fori_loop(0, ROWS, clean, 0, unroll=5)
+    lax.fori_loop(0, ROWS, clean, 0, unroll=10)
     for copy in list(edges.values()) + sky_copies[0] + sky_copies[1]:
         copy.wait_send()
     whole_a.wait_send()

time: 33.8 us -> 33.7 us (level)
  no operation moved by 1% of the time
where the time goes in v11:
time: 33.7 us; the launch traced here: 33.6 us
  Pallas kernels  32.9 us (98%)
  between operations  0.64 us (2%)
    pallas_call x1, Pallas kernels, local(): pl.pallas_call(main_kernel, out_shape=(jax.ShapeDtypeStruct(field, f32),...  31.7 us
    pallas_call x1, Pallas kernels, local(): pl.pallas_call(store_kernel, out_shape=(jax.ShapeDtypeStruct(field, f32),...  1.18 us

profile of v11, /device:TPU:1, one launch (start us, length us, event | category | flops | bytes accessed | tf_op | source)
XLA Modules:
  0.0 33.6 jit_solution(18220772376898115635)
XLA Ops:
  0.6 31.7 %deconvolve.1 = (f32[8,50,2,500]{3,2,1,0:T(2,128)S(1)}, f32[8,128]{1,0:T(8,128)S(1)}) custom-call(f32[8,50,2,500]{3,2,1,0:T(2,128)} %bitcast.6, f32[8,50,2,500]{3,2,1,0:T(2,128)} %bitcast.7, s32[8,50,2,500]{3,2,1,0:T(2,128)} %bitcast.8, f32[8,50,2,500]{3,2,1,0:T(2,128)} %bitcast.9, f32[8,50,2,500]{3,2,1,0:T(2,128)} %bitcast.10, s32[2,40]{1,0:T(2,128)} %index_hbm.1), custom_call_target="tpu_custom_call" | custom-call | tf_op jit(solution)/shard_map/deconvolve/pallas_call | solution.py:360
  32.4 1.2 %store.1 = (f32[8,50,2,500]{3,2,1,0:T(2,128)}, f32[8,50]{1,0:T(8,128)}) custom-call(f32[8,50,2,500]{3,2,1,0:T(2,128)S(1)} %get-tuple-element.6.cleaned, f32[8,128]{1,0:T(8,128)S(1)} %get-tuple-element.7.model), custom_call_target="tpu_custom_call" | custom-call | tf_op jit(solution)/shard_map/store/pallas_call | solution.py:411
